TPU v7x, 32 devices: a whole 2x2x4 slice. The times are simulated.
32 devices in a mesh: fsdp: 8 (over z, x), ckpt: 4 (over y, core).
Axes of the slice: x: 2, y: 2, z: 4, core: 2. Of those that a mesh axis runs over, the one named last changes fastest.
Arguments:
- act_table: bfloat16 [4, 2048, 4096], P('ckpt', 'fsdp'), may hold values from -6 to 6
- token_ids: int32 [4, 2048], P('ckpt'), may hold values from 0 to 2047, each once within a row
- lengths: int32 [4, 8], P('ckpt'), may hold values from 1 to 384, 2048 in all within a row
- grads: bfloat16 [4, 2048, 14336], P('ckpt', 'fsdp'), may hold values from -0.19921875 to 0.19921875
- weights: bfloat16 [4, 8, 4096, 1792], P('ckpt', 'fsdp'), may hold values from -6 to 6
Outputs:
- merged: bfloat16 [8, 4096, 1792], P('fsdp', 'ckpt')
- merge_weight: float32 [8, 4096, 1792], P('fsdp', 'ckpt')
Inputs may be any that keep to these rules, and one draw needn't show every extreme that they name: `token_ids`: each checkpoint's row names every row of the activation table once. One checkpoint's lengths sum to 2048, and one of them is exactly 384.
All inputs are finite; a program needn't handle non-finite values.
Results may differ from a plain program's by a relative error of at most 0.001.
Values may be sent and summed in bfloat16 or wider, within the bound.
No kernel may reach another device: no remote copies, remote signals or barrier semaphores. Data moves between devices by JAX's collectives and lax.ppermute only.
A program may use at most 256 MiB of HBM per device.

v0:
```python
import functools

import jax
import jax.numpy as jnp
from jax import lax
from jax.experimental import pallas as pl
from jax.experimental.pallas import tpu as pltpu
from jax.sharding import PartitionSpec as P


NCB = 8
MOST = 384
LANES = 128
COLS = (256, 128)
ROWS = 256
CUT = 512

prior_mass = 0.1


def swap(value, axis, bit):
    size = lax.axis_size(axis)
    return lax.ppermute(value, axis, [(i, i ^ bit) for i in range(size)])


def slot_kernel(slots, first, last, group_size, window, block, bounds, act, *refs):
    grads, refs = refs[:slots], refs[slots:]
    weights, refs = refs[:slots], refs[slots:]
    den, num = refs[-2:]
    outs, prev = refs[-4:-2], refs[:-4]
    (_, features, tokens), count = act.shape, (bounds.shape[1] - 1) // 2
    step = ROWS if features % ROWS == 0 else features

    def base_of(slot, example):
        base = jnp.minimum((bounds[slot, example] // LANES) * LANES, tokens - window)
        return pl.multiple_of(base, LANES)

    for slot in range(slots):
        examples = []
        for example in range(count):
            begin = bounds[slot, example]
            end = begin + bounds[slot, count + example]
            base = base_of(slot, example)
            place = base + lax.broadcasted_iota(jnp.int32, (window, block), 0)
            rows = grads[slot][pl.ds(base, window), :]
            rows = jnp.where((place >= begin) & (place < end), rows, jnp.zeros_like(rows))
            examples.append((base, rows))
        for low in range(0, features, step):
            part = pl.ds(low, step)
            total = jnp.float32(prior_mass)
            for base, rows in examples:
                mine = act[slot, part, pl.ds(base, window)]
                one = jnp.dot(mine, rows, preferred_element_type=jnp.float32)
                total = total + one * one
            weighted = total * weights[slot][part, :].astype(jnp.float32)
            if slot > 0:
                total, weighted = total + den[part, :], weighted + num[part, :]
            elif not first:
                total, weighted = total + prev[0][part, :], weighted + prev[1][part, :]
            den[part, :] = total
            num[part, :] = weighted

    if last:
        outs[0][...] = (num[...] / den[...]).astype(jnp.bfloat16)
        outs[1][...] = den[...] / group_size
    else:
        outs[0][...] = den[...]
        outs[1][...] = num[...]


def add_slots(bounds, act, at, grads, weights, prev, done, offset, last, group_size):
    slots = len(grads)
    (_, features, tokens), count = act.shape, (bounds.shape[1] - 1) // 2
    span, width = grads[0].shape[1], weights[0].shape[1]
    block = next(b for b in COLS if span % b == 0 and offset % b == 0)
    window = min(-(-(MOST + LANES - 1) // LANES) * LANES, tokens)
    first = prev is None
    skip = offset // block
    chunk = pl.BlockSpec((features, block), lambda j, b: (0, j))
    tile = pl.BlockSpec((features, block), lambda j, b: (0, j + skip))
    whole = pl.BlockSpec(
        (slots, features, tokens), lambda j, b: (at // slots, 0, 0), pipeline_mode=pl.Buffered(1)
    )
    in_specs = [whole]
    in_specs += [pl.BlockSpec((tokens, block), lambda j, b: (0, j))] * slots
    in_specs += [
        pl.BlockSpec((features, block), lambda j, b, s=s: (b[s, 2 * count], j + skip))
        for s in range(slots)
    ]
    operands = [act] + list(grads) + list(weights)
    if not first:
        in_specs += [chunk, chunk]
        operands += list(prev)
    aliases = {}
    if last:
        outs = (
            jax.ShapeDtypeStruct((features, width), jnp.bfloat16),
            jax.ShapeDtypeStruct((features, width), jnp.float32),
        )
        if done is not None:
            aliases = {len(operands) + 1: 0, len(operands) + 2: 1}
            in_specs += [pl.BlockSpec(memory_space=pl.ANY)] * 2
            operands += list(done)
    else:
        outs = (jax.ShapeDtypeStruct((features, span), jnp.float32),) * 2
    return pl.pallas_call(
        functools.partial(slot_kernel, slots, first, last, group_size, window, block),
        out_shape=outs,
        grid_spec=pltpu.PrefetchScalarGridSpec(
            num_scalar_prefetch=1,
            grid=(span // block,),
            in_specs=in_specs,
            out_specs=(tile, tile) if last else (chunk, chunk),
            scratch_shapes=[
                pltpu.VMEM((features, block), jnp.float32),
                pltpu.VMEM((features, block), jnp.float32),
            ],
        ),
        input_output_aliases=aliases,
        cost_estimate=pl.CostEstimate(
            flops=slots * 2 * count * window * features * span,
            bytes_accessed=slots * 2 * (features + span) * tokens + 18 * features * span,
            transcendentals=0,
        ),
    )(bounds, *operands)


def gather_line(own):
    size = lax.axis_size("fsdp")
    n = size // 2

    def send(value, pairs):
        return lax.ppermute(value, "fsdp", pairs)

    line = range(size)
    right, left = [own], [own]
    pair_right = [send(own, [(i, i ^ 1) for i in line])]
    pair_left = [pair_right[0]]
    for k in range(1, n):
        reach = [i for i in line if i // 2 >= k - 1 and i // 2 + 1 < n]
        right.append(send(right[-1], [(i, i + 2) for i in reach]))
        reach = [i for i in line if i // 2 < n - k + 1 and i // 2 >= 1]
        left.append(send(left[-1], [(i, i - 2) for i in reach]))
        pair_right.append(send(right[-1], [(i, i ^ 1) for i in line if i // 2 >= k]))
        pair_left.append(send(left[-1], [(i, i ^ 1) for i in line if i // 2 < n - k]))
    return right, left, pair_right, pair_left


def permute_kernel(n, where, ids, *refs):
    sources, (out, table, sems) = refs[:-3], refs[-3:]
    right, left = sources[:n], sources[n:2 * n - 1]
    pair_right, pair_left = sources[2 * n - 1:3 * n - 1], sources[3 * n - 1:]
    slot, step = pl.program_id(0), pl.program_id(1)
    z, x = where[0], where[1]

    def place(k, s):
        return lax.rem(z - k + n, n) * 2 + (x if s == 0 else 1 - x)

    def copy(source, part, k, s):
        return pltpu.make_async_copy(source.at[part], table.at[part, place(k, s)], sems.at[part, k, s])

    @pl.when((slot == 0) & (step == 0))
    def _():
        for part in range(2):
            for s, ups, downs in ((0, right, left), (1, pair_right, pair_left)):
                copy(ups[0], part, 0, s).start()
                for k in range(1, n):
                    @pl.when(z >= k)
                    def _():
                        copy(ups[k], part, k, s).start()

                    @pl.when(z < k)
                    def _():
                        copy(downs[n - k - 1], part, k, s).start()

    for part in range(2):
        @pl.when((slot == part) & (step == 0))
        def _():
            for k in range(n):
                for s in range(2):
                    copy(right[0], part, k, s).wait()

    rows = table[slot].reshape(-1, table.shape[-1])
    width = min(ROWS, ids.shape[1])
    for low in range(0, ids.shape[1], width):
        mine = ids[0, low:low + width]
        hot = lax.broadcasted_iota(jnp.int32, (width, rows.shape[0]), 1) == mine
        hot = jnp.where(hot, jnp.float32(1), jnp.float32(0)).astype(rows.dtype)
        picked = jnp.dot(hot, rows, preferred_element_type=jnp.float32).astype(rows.dtype)
        out[0, :, low:low + width] = picked.T


def permute_pair(ids, pieces):
    right, left, pair_right, pair_left = pieces
    n = len(right)
    _, local, features = right[0].shape
    tokens = ids.shape[1]
    rows = min(2 * ROWS, tokens)
    me = lax.axis_index("fsdp")
    where = jnp.stack([me // 2, me % 2]).astype(jnp.int32)
    operands = [*right, *left[1:], *pair_right, *pair_left[1:]]
    return pl.pallas_call(
        functools.partial(permute_kernel, n),
        out_shape=jax.ShapeDtypeStruct((2, features, tokens), right[0].dtype),
        grid_spec=pltpu.PrefetchScalarGridSpec(
            num_scalar_prefetch=1,
            grid=(2, tokens // rows),
            in_specs=[pl.BlockSpec((1, rows, 1), lambda p, t, w: (p, t, 0))]
            + [pl.BlockSpec(memory_space=pl.ANY)] * len(operands),
            out_specs=pl.BlockSpec((1, features, rows), lambda p, t, w: (p, 0, t)),
            scratch_shapes=[
                pltpu.VMEM((2, 2 * n, local, features), right[0].dtype),
                pltpu.SemaphoreType.DMA((2, n, 2)),
            ],
        ),
        cost_estimate=pl.CostEstimate(
            flops=4 * tokens * tokens * features, bytes_accessed=8 * tokens * features, transcendentals=0
        ),
    )(where, ids[:, :, None], *operands)


def permuted(rows, place):
    hot = (lax.broadcasted_iota(jnp.int32, (rows.shape[0], place.shape[0]), 0) == place[None, :])
    return lax.dot_general(
        rows, hot.astype(rows.dtype), (((0,), (0,)), ((), ())), preferred_element_type=jnp.float32
    ).astype(rows.dtype)


def body(act_table, token_ids, lengths, grads, weights):
    group = lax.axis_size("fsdp")
    size = lax.axis_size("ckpt")
    c = lax.axis_index("ckpt")
    y, core = c // 2, c % 2
    row_blocks = group // NCB
    own_rows, own_grads, own_weight = act_table[0], grads[0], weights[0, 0]
    local, depth = own_rows.shape
    tokens = token_ids.shape[1]
    features = depth // row_blocks // size

    starts = jnp.cumsum(lengths[0]) - lengths[0]
    meta = jnp.concatenate([starts, lengths[0], token_ids[0]]).astype(jnp.int32)
    metas = [meta, swap(meta, "ckpt", 1), swap(meta, "ckpt", 2), swap(meta, "ckpt", 3)]
    count = lengths.shape[1]

    parts = own_rows.reshape(local, row_blocks, size, features)
    half = 2

    def quarter(value, index):
        return lax.dynamic_index_in_dim(value, index, 2, keepdims=False)

    far = lax.dynamic_slice_in_dim(parts, (1 - y) * half, half, 2)
    far = swap(far, "ckpt", 2)
    near = lax.dynamic_slice_in_dim(parts, y * half, half, 2)
    act0, act2 = quarter(near, core), quarter(far, core)
    act1 = swap(quarter(near, 1 - core), "ckpt", 1)
    act3 = swap(quarter(far, 1 - core), "ckpt", 1)

    far_w = lax.dynamic_slice_in_dim(own_weight, (1 - y) * 2 * features, 2 * features, 0)
    far_w = swap(far_w, "ckpt", 2)

    def rows_of(value, index):
        return lax.dynamic_slice_in_dim(value, index * features, features, 0)

    weight1 = swap(rows_of(own_weight, y * 2 + 1 - core), "ckpt", 1)
    weight3 = swap(rows_of(far_w, 1 - core), "ckpt", 1)
    weight_slots = (own_weight, weight1, far_w, weight3)
    weight_rows = (c, 0, core, 0)

    width = own_grads.shape[1] // NCB
    cut = min(-(-(width // 2) // CUT) * CUT, width - LANES)
    chunks = ((0, cut), (cut, width))
    grad_slots, previous = [], None
    for low, high in chunks:
        piece = own_grads.reshape(local, NCB, width)[:, :, low:high]
        piece = jnp.transpose(piece, (1, 0, 2))
        if row_blocks > 1:
            piece = jnp.broadcast_to(piece[None], (row_blocks,) + piece.shape)
            piece = piece.reshape(group, local, high - low)
        if previous is not None:
            piece, previous = lax.optimization_barrier((piece, previous))
            grad_slots[-1][0] = previous
        grad0 = lax.all_to_all(piece, "fsdp", split_axis=0, concat_axis=0, tiled=True)
        grad0 = grad0.reshape(tokens, high - low)
        previous = grad0
        grad_slots.append([grad0, None, None, None])
    for slots in grad_slots:
        slots[2] = swap(slots[0], "ckpt", 2)
        slots[1] = swap(slots[0], "ckpt", 1)
        slots[3] = swap(slots[2], "ckpt", 1)

    ids = [m[2 * count:] for m in metas]

    def gathered(a, b, pair_ids):
        if row_blocks == 1:
            pieces = gather_line(jnp.stack([a[:, 0], b[:, 0]]))
            return permute_pair(jnp.stack(pair_ids), pieces)
        both = jnp.stack([a, b])
        both = jnp.transpose(both, (2, 0, 1, 3))[:, None]
        both = jnp.broadcast_to(both, (row_blocks, NCB, 2, local, features))
        both = both.reshape(group, 2, local, features)
        table = lax.all_to_all(both, "fsdp", split_axis=0, concat_axis=0, tiled=True)
        tables = (table[:, 0].reshape(tokens, features), table[:, 1].reshape(tokens, features))
        return jnp.stack([permuted(rows, place) for rows, place in zip(tables, pair_ids)])

    near_acts = gathered(act0, act1, ids[:2])
    far_acts = gathered(act2, act3, ids[2:])
    bounds = jnp.stack(
        [jnp.append(m[:2 * count], jnp.int32(row)) for m, row in zip(metas, weight_rows)]
    )
    plan = ((0, 1), (2, 3))
    done = None
    for index, (low, high) in enumerate(chunks):
        carry = None
        for slots in plan:
            last = slots[-1] == size - 1
            take = lambda values: [values[j] for j in slots]
            carry = add_slots(
                bounds[slots[0]:slots[-1] + 1], near_acts if slots[0] < 2 else far_acts,
                slots[0] % 2, take(grad_slots[index]), take(weight_slots), carry, done, low, last, size,
            )
        done = carry
    merged, merge_weight = done
    return merged[None], merge_weight[None]


def solution(mesh):
    placed = (
        P("ckpt", "fsdp", None),
        P("ckpt", None),
        P("ckpt", None),
        P("ckpt", "fsdp", None),
        P("ckpt", "fsdp", None, None),
    )
    return jax.shard_map(
        body,
        mesh=mesh,
        in_specs=placed,
        out_specs=(P("fsdp", "ckpt", None), P("fsdp", "ckpt", None)),
        check_vma=False,
    )
```

profile of v0, /device:TPU:0, one launch (start us, length us, event | category | flops | bytes accessed | tf_op | source)
XLA Modules:
  0.0 540.1 jit_solution(17330873787917982255)
XLA Ops:
  0.6 5.2 copy.26
  6.4 2.5 copy-done
  8.9 4.3 copy.31
  13.1 7.3 %all-to-all-start = ((bf16[8,256,1024]{2,1,0:T(8,128)(2,1)}), bf16[8,256,1024]{2,1,0:T(8,128)(2,1)}, u32[]{:S(2)}, u32[]{:S(2)}) async-start(bf16[8,256,1024]{2,1,0:T(8,128)(2,1)} %bitcast.57), calls=%async_computation | async-start | bytes 8388608 | tf_op jit(solution)/shard_map/all_to_all | solution.py:282
  20.4 3.3 reshape_squeeze.7
  23.7 2.2 constant_dynamic-slice_fusion.1
  25.9 1.0 copy.33
  26.9 1.1 constant_dynamic-slice_fusion.3
  28.2 1.6 collective-permute-start.2
  30.9 1.1 pad_maximum_fusion.1.refs_0_
  32.1 2.1 collective-permute-start.29
  34.2 1.3 collective-permute-start.26
  35.5 4.6 collective-permute-start.23
  40.1 6.5 %dynamic-slice_bitcast_fusion = bf16[2048,1792]{1,0:T(8,128)(2,1)} fusion(bf16[1,1,4096,1792]{3,2,1,0:T(8,128)(2,1)} %param.9, s32[]{:T(128)S(6)} %select_n.58), kind=kLoop, calls=%fused_computation | loop fusion | bytes 14680068 | tf_op jit(solution)/shard_map/dynamic_slice | solution.py:258
  46.6 7.1 %collective-permute-done.1 = s32[2064]{0:T(1024)S(1)} collective-permute-done((s32[2064]{0:T(1024)S(1)}, s32[2064]{0:T(1024)S(1)}, u32[]{:S(2)}, u32[]{:S(2)}) %collective-permute-start.1) | collective-permute-done | bytes 8288 | tf_op jit(solution)/shard_map/ppermute | solution.py:23
  53.7 1.5 collective-permute-start
  55.7 1.3 dynamic-slice_bitcast_fusion.3
  57.4 34.3 %collective-permute-done.26.refs_4_ = bf16[2,256,1024]{2,1,0:T(8,128)(2,1)S(1)} collective-permute-done((bf16[2,256,1024]{2,1,0:T(8,128)(2,1)S(1)}, bf16[2,256,1024]{2,1,0:T(8,128)(2,1)S(1)}, u32[]{:S(2)}, u32[]{:S(2)}) %collective-permute-start.26) | collective-permute-done | bytes 1048608 | tf_op jit(solution)/shard_map/ppermute | solution.py:133
  91.7 13.2 %collective-permute-start.33 = (bf16[2,256,1024]{2,1,0:T(8,128)(2,1)S(1)}, bf16[2,256,1024]{2,1,0:T(8,128)(2,1)S(1)}, u32[]{:S(2)}, u32[]{:S(2)}) collective-permute-start(bf16[2,256,1024]{2,1,0:T(8,128)(2,1)S(1)} %collective-permute-done.26.refs_4_), channel_id=1, source_target_pairs={{0,4},{4,0},{8,12},{12,8},{16,20},{20,16},{1,5},{5,1},{9,13},{13,9... | collective-permute-start | bytes 3145736 | tf_op jit(solution)/shard_map/ppermute | solution.py:133
  104.9 1.3 collective-permute-start.27
  106.2 5.3 collective-permute-done.23.refs_1_
  112.3 0.9 collective-permute-start.24
  113.2 1.1 pad_maximum_fusion.refs_0_
  114.3 13.1 %collective-permute-done.33.refs_11_ = bf16[2,256,1024]{2,1,0:T(8,128)(2,1)S(1)} collective-permute-done((bf16[2,256,1024]{2,1,0:T(8,128)(2,1)S(1)}, bf16[2,256,1024]{2,1,0:T(8,128)(2,1)S(1)}, u32[]{:S(2)}, u32[]{:S(2)}) %collective-permute-start.33) | collective-permute-done | bytes 1048608 | tf_op jit(solution)/shard_map/ppermute | solution.py:133
  127.3 1.7 collective-permute-start.10
  129.1 35.2 %collective-permute-done.27.refs_5_ = bf16[2,256,1024]{2,1,0:T(8,128)(2,1)} collective-permute-done((bf16[2,256,1024]{2,1,0:T(8,128)(2,1)S(1)}, bf16[2,256,1024]{2,1,0:T(8,128)(2,1)}, u32[]{:S(2)}, u32[]{:S(2)}) %collective-permute-start.27) | collective-permute-done | bytes 1048608 | tf_op jit(solution)/shard_map/ppermute | solution.py:133
  164.3 1.3 collective-permute-start.7
  165.6 24.3 %collective-permute-start.4 = (bf16[2,256,1024]{2,1,0:T(8,128)(2,1)}, bf16[2,256,1024]{2,1,0:T(8,128)(2,1)}, u32[]{:S(2)}, u32[]{:S(2)}) collective-permute-start(bf16[2,256,1024]{2,1,0:T(8,128)(2,1)} %pad_maximum_fusion.refs_0_), channel_id=1, source_target_pairs={{0,8},{4,12},{8,16},{12,20},{16,24},{20,28},{1,9},{5,13},{9,17},{1... | collective-permute-start | bytes 3145736 | tf_op jit(solution)/shard_map/ppermute | solution.py:133
  189.9 3.4 collective-permute-start.34
  193.3 2.1 slice.44
  195.4 2.3 copy.32
  197.7 3.6 all-to-all-start.1
  201.4 1.3 collective-permute-start.28
  203.5 9.3 %collective-permute-done.4.refs_1_ = bf16[2,256,1024]{2,1,0:T(8,128)(2,1)} collective-permute-done((bf16[2,256,1024]{2,1,0:T(8,128)(2,1)}, bf16[2,256,1024]{2,1,0:T(8,128)(2,1)}, u32[]{:S(2)}, u32[]{:S(2)}) %collective-permute-start.4) | collective-permute-done | bytes 1048608 | tf_op jit(solution)/shard_map/ppermute | solution.py:133
  213.5 23.4 %collective-permute-done.34.refs_12_ = bf16[2,256,1024]{2,1,0:T(8,128)(2,1)} collective-permute-done((bf16[2,256,1024]{2,1,0:T(8,128)(2,1)}, bf16[2,256,1024]{2,1,0:T(8,128)(2,1)}, u32[]{:S(2)}, u32[]{:S(2)}) %collective-permute-start.34) | collective-permute-done | bytes 1048608 | tf_op jit(solution)/shard_map/ppermute | solution.py:133
  236.9 4.4 collective-permute-start.14
  241.3 36.7 %collective-permute-done.28.refs_6_ = bf16[2,256,1024]{2,1,0:T(8,128)(2,1)S(1)} collective-permute-done((bf16[2,256,1024]{2,1,0:T(8,128)(2,1)}, bf16[2,256,1024]{2,1,0:T(8,128)(2,1)S(1)}, u32[]{:S(2)}, u32[]{:S(2)}) %collective-permute-start.28) | collective-permute-done | bytes 1048608 | tf_op jit(solution)/shard_map/ppermute | solution.py:133
  277.9 1.3 collective-permute-start.8
  280.0 1.6 collective-permute-start.38
  281.6 1.6 collective-permute-start.5
  283.2 12.7 %collective-permute-done.8.refs_5_ = bf16[2,256,1024]{2,1,0:T(8,128)(2,1)} collective-permute-done((bf16[2,256,1024]{2,1,0:T(8,128)(2,1)}, bf16[2,256,1024]{2,1,0:T(8,128)(2,1)}, u32[]{:S(2)}, u32[]{:S(2)}) %collective-permute-start.8) | collective-permute-done | bytes 1048608 | tf_op jit(solution)/shard_map/ppermute | solution.py:133
  295.9 3.3 collective-permute-start.35
  300.0 2.5 collective-permute-start.15
  302.5 21.3 %collective-permute-done.35.refs_13_ = bf16[2,256,1024]{2,1,0:T(8,128)(2,1)S(1)} collective-permute-done((bf16[2,256,1024]{2,1,0:T(8,128)(2,1)S(1)}, bf16[2,256,1024]{2,1,0:T(8,128)(2,1)S(1)}, u32[]{:S(2)}, u32[]{:S(2)}) %collective-permute-start.35) | collective-permute-done | bytes 1048608 | tf_op jit(solution)/shard_map/ppermute | solution.py:133
  323.8 1.3 collective-permute-start.9
  325.2 1.7 collective-permute-start.6
  326.8 10.0 %collective-permute-done.15.refs_12_ = bf16[2,256,1024]{2,1,0:T(8,128)(2,1)S(1)} collective-permute-done((bf16[2,256,1024]{2,1,0:T(8,128)(2,1)}, bf16[2,256,1024]{2,1,0:T(8,128)(2,1)S(1)}, u32[]{:S(2)}, u32[]{:S(2)}) %collective-permute-start.15) | collective-permute-done | bytes 1048608 | tf_op jit(solution)/shard_map/ppermute | solution.py:133
  336.8 1.0 copy-done.17
  337.8 1.6 collective-permute-start.12
  340.2 4.1 dynamic-slice_bitcast_fusion.1
  344.9 3.6 collective-permute-start.16
  348.6 1.7 collective-permute-start.13
  351.3 2.0 copy.15.ids
  353.2 2.1 copy.20.ids
  355.9 4.1 constant_dynamic-slice_fusion.2
  360.0 3.2 collective-permute-done.16.refs_13_
  363.7 1.6 collective-permute-start.17
  365.3 25.0 %shard_map.69.act = bf16[2,1024,2048]{2,1,0:T(8,128)(2,1)} custom-call(s32[2]{0:T(128)} %pad_add_fusion.4.where, s32[2,2048,1]{2,1,0:T(8,128)} %copy.20.ids, bf16[2,256,1024]{2,1,0:T(8,128)(2,1)} %copy-done.2, bf16[2,256,1024]{2,1,0:T(8,128)(2,1)} %copy-done.7, bf16[2,256,1024]{2,1,0:T(8,128)(2,1)} %copy-done.10, bf16[2,256,1024]{2,1,0:T(8,128)(2,1)} %copy-done.14, ...), custom_call_target="tpu_custom_call" | custom-call | flops 17179869184 | bytes 16777216 | tf_op jit(solution)/shard_map/pallas_call | solution.py:202
  390.3 25.0 %shard_map.68.act = bf16[2,1024,2048]{2,1,0:T(8,128)(2,1)} custom-call(s32[2]{0:T(128)} %pad_add_fusion.4.where, s32[2,2048,1]{2,1,0:T(8,128)} %copy.15.ids, bf16[2,256,1024]{2,1,0:T(8,128)(2,1)} %pad_maximum_fusion.refs_0_, bf16[2,256,1024]{2,1,0:T(8,128)(2,1)} %collective-permute-done.4.refs_1_, bf16[2,256,1024]{2,1,0:T(8,128)(2,1)} %collective-permute-done.5.refs_2_, ...), custom_call_target="tpu_custom_call" | custom-call | flops 17179869184 | bytes 16777216 | tf_op jit(solution)/shard_map/pallas_call | solution.py:202
  415.4 18.6 %collective-permute-done.17.refs_0_ = bf16[2048,768]{1,0:T(8,128)(2,1)} collective-permute-done((bf16[2048,768]{1,0:T(8,128)(2,1)S(1)}, bf16[2048,768]{1,0:T(8,128)(2,1)}, u32[]{:S(2)}, u32[]{:S(2)}) %collective-permute-start.17) | collective-permute-done | bytes 3145760 | tf_op jit(solution)/shard_map/ppermute | solution.py:23
  433.9 28.6 %shard_map.71 = (f32[1024,1024]{1,0:T(8,128)}, f32[1024,1024]{1,0:T(8,128)}) custom-call(s32[2,17]{1,0:T(2,128)} %pad_add_fusion.1.bounds, bf16[2,1024,2048]{2,1,0:T(8,128)(2,1)} %shard_map.69.act, bf16[2048,1024]{1,0:T(8,128)(2,1)} %bitcast.17.refs_0_, bf16[2048,1024]{1,0:T(8,128)(2,1)} %collective-permute-done.40.refs_1_, bf16[4096,1792]{1,0:T(8,128)(2,1)} %bitcast.58, ...), custom_call_target="tpu_custom_call" | custom-call | flops 17179869184 | bytes 35651584 | tf_op jit(solution)/shard_map/pallas_call | solution.py:106
  462.5 29.7 %shard_map.72 = (bf16[1024,1792]{1,0:T(8,128)(2,1)}, f32[1024,1792]{1,0:T(8,128)}) custom-call(s32[2,17]{1,0:T(2,128)} %pad_add_fusion.bounds, bf16[2,1024,2048]{2,1,0:T(8,128)(2,1)} %shard_map.68.act, bf16[2048,1024]{1,0:T(8,128)(2,1)} %collective-permute-done.38.refs_0_, bf16[2048,1024]{1,0:T(8,128)(2,1)} %collective-permute-done.39.refs_1_, ...), custom_call_target="tpu_custom_call" | custom-call | flops 17179869184 | bytes 35651584 | tf_op jit(solution)/shard_map/pallas_call | solution.py:106
  492.2 23.2 %shard_map.70 = (f32[1024,768]{1,0:T(8,128)}, f32[1024,768]{1,0:T(8,128)}) custom-call(s32[2,17]{1,0:T(2,128)} %pad_add_fusion.1.bounds, bf16[2,1024,2048]{2,1,0:T(8,128)(2,1)} %shard_map.69.act, bf16[2048,768]{1,0:T(8,128)(2,1)} %bitcast.63, bf16[2048,768]{1,0:T(8,128)(2,1)} %collective-permute-done.36.refs_1_, bf16[4096,1792]{1,0:T(8,128)(2,1)} %bitcast.59, ...), custom_call_target="tpu_custom_call" | custom-call | flops 12884901888 | bytes 28835840 | tf_op jit(solution)/shard_map/pallas_call | solution.py:106
  515.4 24.3 %shard_map.73 = (bf16[1024,1792]{1,0:T(8,128)(2,1)}, f32[1024,1792]{1,0:T(8,128)}) custom-call(s32[2,17]{1,0:T(2,128)} %pad_add_fusion.bounds, bf16[2,1024,2048]{2,1,0:T(8,128)(2,1)} %shard_map.68.act, bf16[2048,768]{1,0:T(8,128)(2,1)} %collective-permute-done.17.refs_0_, ...), custom_call_target="tpu_custom_call", output_to_operand_aliasing={{0}: (8, {}), {1}: (9, {})} | custom-call | flops 12884901888 | bytes 28835840 | tf_op jit(solution)/shard_map/pallas_call | solution.py:106
  (103 shorter events, 10.1 us)
Async XLA Ops:
  5.8 3.1 copy-start
  13.1 184.6 %all-to-all-start = ((bf16[8,256,1024]{2,1,0:T(8,128)(2,1)}), bf16[8,256,1024]{2,1,0:T(8,128)(2,1)}, u32[]{:S(2)}, u32[]{:S(2)}) async-start(bf16[8,256,1024]{2,1,0:T(8,128)(2,1)} %bitcast.57), calls=%async_computation | async-start | bytes 8388608 | tf_op jit(solution)/shard_map/all_to_all | solution.py:282
  25.9 3.9 copy-start.4
  25.9 4.1 copy-start.3
  26.9 4.0 collective-permute-start.22
  28.2 27.0 %collective-permute-start.2 = (bf16[256,1,2,1024]{3,0,2,1:T(8,128)(2,1)S(1)}, bf16[256,1,2,1024]{3,0,2,1:T(8,128)(2,1)}, u32[]{:S(2)}, u32[]{:S(2)}) collective-permute-start(bf16[256,1,2,1024]{3,0,2,1:T(8,128)(2,1)S(1)} %copy.21), channel_id=1, source_target_pairs={{0,2},{1,3},{2,0},{3,1},{4,6},{5,7},{6,4},{7,5},{8,10},{9,11},{10,... | collective-permute-start | bytes 3145736 | tf_op jit(solution)/shard_map/ppermute | solution.py:23
  30.1 5.3 collective-permute-start.21
  30.3 23.3 %collective-permute-start.1 = (s32[2064]{0:T(1024)S(1)}, s32[2064]{0:T(1024)S(1)}, u32[]{:S(2)}, u32[]{:S(2)}) collective-permute-start(s32[2064]{0:T(1024)S(1)} %concatenate.20), channel_id=1, source_target_pairs={{0,3},{1,2},{2,1},{3,0},{4,7},{5,6},{6,5},{7,4},{8,11},{9,10},{10,... | collective-permute-start | bytes 24776 | tf_op jit(solution)/shard_map/ppermute | solution.py:23
  32.1 14.5 %copy-start.2 = (bf16[2,256,1024]{2,1,0:T(8,128)(2,1)}, bf16[2,256,1024]{2,1,0:T(8,128)(2,1)S(1)}, u32[]{:S(2)}) copy-start(bf16[2,256,1024]{2,1,0:T(8,128)(2,1)S(1)} %pad_maximum_fusion.1.refs_0_) | copy-start | bytes 3145732
  32.1 72.8 %collective-permute-start.29 = (bf16[2,256,1024]{2,1,0:T(8,128)(2,1)S(1)}, bf16[2,256,1024]{2,1,0:T(8,128)(2,1)S(1)}, u32[]{:S(2)}, u32[]{:S(2)}) collective-permute-start(bf16[2,256,1024]{2,1,0:T(8,128)(2,1)S(1)} %pad_maximum_fusion.1.refs_0_), channel_id=1, source_target_pairs={{0,4},{4,0},{8,12},{12,8},{16,20},{20,16},{24,28},{28,24},{1,5},{5... | collective-permute-start | bytes 3145736 | tf_op jit(solution)/shard_map/ppermute | solution.py:133
  34.2 57.6 %collective-permute-start.26 = (bf16[2,256,1024]{2,1,0:T(8,128)(2,1)S(1)}, bf16[2,256,1024]{2,1,0:T(8,128)(2,1)S(1)}, u32[]{:S(2)}, u32[]{:S(2)}) collective-permute-start(bf16[2,256,1024]{2,1,0:T(8,128)(2,1)S(1)} %pad_maximum_fusion.1.refs_0_), channel_id=1, source_target_pairs={{8,0},{12,4},{16,8},{20,12},{24,16},{28,20},{9,1},{13,5},{17,9},{2... | collective-permute-start | bytes 3145736 | tf_op jit(solution)/shard_map/ppermute | solution.py:133
  35.5 76.1 %collective-permute-start.23 = (bf16[2,256,1024]{2,1,0:T(8,128)(2,1)S(1)}, bf16[2,256,1024]{2,1,0:T(8,128)(2,1)S(1)}, u32[]{:S(2)}, u32[]{:S(2)}) collective-permute-start(bf16[2,256,1024]{2,1,0:T(8,128)(2,1)S(1)} %pad_maximum_fusion.1.refs_0_), channel_id=1, source_target_pairs={{0,8},{4,12},{8,16},{12,20},{16,24},{20,28},{1,9},{5,13},{9,17},{1... | collective-permute-start | bytes 3145736 | tf_op jit(solution)/shard_map/ppermute | solution.py:133
  53.7 3.7 collective-permute-start
  55.2 295.4 %collective-permute-start.19 = (bf16[2048,1792]{1,0:T(8,128)(2,1)}, bf16[2048,1792]{1,0:T(8,128)(2,1)}, u32[]{:S(2)}, u32[]{:S(2)}) collective-permute-start(bf16[2048,1792]{1,0:T(8,128)(2,1)} %dynamic-slice_bitcast_fusion), channel_id=1, source_target_pairs={{0,2},{1,3},{2,0},{3,1},{4,6},{5,7},{6,4},{7,5},{8,10},{9,11},{10,... | collective-permute-start | bytes 22020104 | tf_op jit(solution)/shard_map/ppermute | solution.py:23
  57.4 54.9 %collective-permute-start.3 = (bf16[256,1,1024]{2,0,1:T(8,128)(2,1)S(1)}, bf16[256,1,1024]{2,0,1:T(8,128)(2,1)S(1)}, u32[]{:S(2)}, u32[]{:S(2)}) collective-permute-start(bf16[256,1,1024]{2,0,1:T(8,128)(2,1)S(1)} %get-tuple-element.25), channel_id=1, source_target_pairs={{0,1},{1,0},{2,3},{3,2},{4,5},{5,4},{6,7},{7,6},{8,9},{9,8},{10,11... | collective-permute-start | bytes 1572872 | tf_op jit(solution)/shard_map/ppermute | solution.py:23
  91.7 103.7 %copy-start.6 = (bf16[2,256,1024]{2,1,0:T(8,128)(2,1)}, bf16[2,256,1024]{2,1,0:T(8,128)(2,1)S(1)}, u32[]{:S(2)}) copy-start(bf16[2,256,1024]{2,1,0:T(8,128)(2,1)S(1)} %collective-permute-done.26.refs_4_) | copy-start | bytes 3145732
  91.7 35.6 %collective-permute-start.33 = (bf16[2,256,1024]{2,1,0:T(8,128)(2,1)S(1)}, bf16[2,256,1024]{2,1,0:T(8,128)(2,1)S(1)}, u32[]{:S(2)}, u32[]{:S(2)}) collective-permute-start(bf16[2,256,1024]{2,1,0:T(8,128)(2,1)S(1)} %collective-permute-done.26.refs_4_), channel_id=1, source_target_pairs={{0,4},{4,0},{8,12},{12,8},{16,20},{20,16},{1,5},{5,1},{9,13},{13,9... | collective-permute-start | bytes 3145736 | tf_op jit(solution)/shard_map/ppermute | solution.py:133
  104.9 90.5 %copy-start.5 = (bf16[2,256,1024]{2,1,0:T(8,128)(2,1)}, bf16[2,256,1024]{2,1,0:T(8,128)(2,1)S(1)}, u32[]{:S(2)}) copy-start(bf16[2,256,1024]{2,1,0:T(8,128)(2,1)S(1)} %collective-permute-done.29.refs_7_) | copy-start | bytes 3145732
  104.9 59.3 %collective-permute-start.27 = (bf16[2,256,1024]{2,1,0:T(8,128)(2,1)S(1)}, bf16[2,256,1024]{2,1,0:T(8,128)(2,1)}, u32[]{:S(2)}, u32[]{:S(2)}) collective-permute-start(bf16[2,256,1024]{2,1,0:T(8,128)(2,1)S(1)} %collective-permute-done.26.refs_4_), channel_id=1, source_target_pairs={{8,0},{12,4},{16,8},{20,12},{9,1},{13,5},{17,9},{21,13},{10,2},{14... | collective-permute-start | bytes 3145736 | tf_op jit(solution)/shard_map/ppermute | solution.py:133
  111.6 83.8 %copy-start.7 = (bf16[2,256,1024]{2,1,0:T(8,128)(2,1)}, bf16[2,256,1024]{2,1,0:T(8,128)(2,1)S(1)}, u32[]{:S(2)}) copy-start(bf16[2,256,1024]{2,1,0:T(8,128)(2,1)S(1)} %collective-permute-done.23.refs_1_) | copy-start | bytes 3145732
  111.6 54.0 %collective-permute-start.30 = (bf16[2,256,1024]{2,1,0:T(8,128)(2,1)S(1)}, bf16[2,256,1024]{2,1,0:T(8,128)(2,1)S(1)}, u32[]{:S(2)}, u32[]{:S(2)}) collective-permute-start(bf16[2,256,1024]{2,1,0:T(8,128)(2,1)S(1)} %collective-permute-done.23.refs_1_), channel_id=1, source_target_pairs={{8,12},{12,8},{16,20},{20,16},{24,28},{28,24},{9,13},{13,9},{17,21... | collective-permute-start | bytes 3145736 | tf_op jit(solution)/shard_map/ppermute | solution.py:133
  112.3 77.6 %collective-permute-start.24 = (bf16[2,256,1024]{2,1,0:T(8,128)(2,1)S(1)}, bf16[2,256,1024]{2,1,0:T(8,128)(2,1)S(1)}, u32[]{:S(2)}, u32[]{:S(2)}) collective-permute-start(bf16[2,256,1024]{2,1,0:T(8,128)(2,1)S(1)} %collective-permute-done.23.refs_1_), channel_id=1, source_target_pairs={{8,16},{12,20},{16,24},{20,28},{9,17},{13,21},{17,25},{21,29},{10,... | collective-permute-start | bytes 3145736 | tf_op jit(solution)/shard_map/ppermute | solution.py:133
  127.3 62.5 %copy-start.8 = (bf16[2,256,1024]{2,1,0:T(8,128)(2,1)}, bf16[2,256,1024]{2,1,0:T(8,128)(2,1)S(1)}, u32[]{:S(2)}) copy-start(bf16[2,256,1024]{2,1,0:T(8,128)(2,1)S(1)} %collective-permute-done.33.refs_11_) | copy-start | bytes 3145732
  127.3 74.1 %collective-permute-start.10 = (bf16[2,256,1024]{2,1,0:T(8,128)(2,1)}, bf16[2,256,1024]{2,1,0:T(8,128)(2,1)}, u32[]{:S(2)}, u32[]{:S(2)}) collective-permute-start(bf16[2,256,1024]{2,1,0:T(8,128)(2,1)} %pad_maximum_fusion.refs_0_), channel_id=1, source_target_pairs={{0,4},{4,0},{8,12},{12,8},{16,20},{20,16},{24,28},{28,24},{1,5},{5... | collective-permute-start | bytes 3145736 | tf_op jit(solution)/shard_map/ppermute | solution.py:133
  164.3 38.4 %collective-permute-start.7 = (bf16[2,256,1024]{2,1,0:T(8,128)(2,1)}, bf16[2,256,1024]{2,1,0:T(8,128)(2,1)}, u32[]{:S(2)}, u32[]{:S(2)}) collective-permute-start(bf16[2,256,1024]{2,1,0:T(8,128)(2,1)} %pad_maximum_fusion.refs_0_), channel_id=1, source_target_pairs={{8,0},{12,4},{16,8},{20,12},{24,16},{28,20},{9,1},{13,5},{17,9},{2... | collective-permute-start | bytes 3145736 | tf_op jit(solution)/shard_map/ppermute | solution.py:133
  165.6 27.7 %copy-start.9 = (bf16[2,256,1024]{2,1,0:T(8,128)(2,1)}, bf16[2,256,1024]{2,1,0:T(8,128)(2,1)S(1)}, u32[]{:S(2)}) copy-start(bf16[2,256,1024]{2,1,0:T(8,128)(2,1)S(1)} %collective-permute-done.30.refs_8_) | copy-start | bytes 3145732
  165.6 47.2 %collective-permute-start.4 = (bf16[2,256,1024]{2,1,0:T(8,128)(2,1)}, bf16[2,256,1024]{2,1,0:T(8,128)(2,1)}, u32[]{:S(2)}, u32[]{:S(2)}) collective-permute-start(bf16[2,256,1024]{2,1,0:T(8,128)(2,1)} %pad_maximum_fusion.refs_0_), channel_id=1, source_target_pairs={{0,8},{4,12},{8,16},{12,20},{16,24},{20,28},{1,9},{5,13},{9,17},{1... | collective-permute-start | bytes 3145736 | tf_op jit(solution)/shard_map/ppermute | solution.py:133
  189.9 5.5 %copy-start.10 = (bf16[2,256,1024]{2,1,0:T(8,128)(2,1)}, bf16[2,256,1024]{2,1,0:T(8,128)(2,1)S(1)}, u32[]{:S(2)}) copy-start(bf16[2,256,1024]{2,1,0:T(8,128)(2,1)S(1)} %collective-permute-done.24.refs_2_) | copy-start | bytes 3145732
  189.9 47.0 %collective-permute-start.34 = (bf16[2,256,1024]{2,1,0:T(8,128)(2,1)}, bf16[2,256,1024]{2,1,0:T(8,128)(2,1)}, u32[]{:S(2)}, u32[]{:S(2)}) collective-permute-start(bf16[2,256,1024]{2,1,0:T(8,128)(2,1)} %collective-permute-done.27.refs_5_), channel_id=1, source_target_pairs={{0,4},{4,0},{8,12},{12,8},{1,5},{5,1},{9,13},{13,9},{2,6},{6,2},{1... | collective-permute-start | bytes 3145736 | tf_op jit(solution)/shard_map/ppermute | solution.py:133
  197.7 166.0 %all-to-all-start.1 = ((bf16[8,256,768]{2,1,0:T(8,128)(2,1)}), bf16[8,256,768]{2,1,0:T(8,128)(2,1)S(1)}, u32[]{:S(2)}, u32[]{:S(2)}) async-start(bf16[8,256,768]{2,1,0:T(8,128)(2,1)} %bitcast.52), calls=%async_computation.1 | async-start | bytes 6291456 | tf_op jit(solution)/shard_map/all_to_all | solution.py:282
  201.4 76.5 %collective-permute-start.28 = (bf16[2,256,1024]{2,1,0:T(8,128)(2,1)}, bf16[2,256,1024]{2,1,0:T(8,128)(2,1)S(1)}, u32[]{:S(2)}, u32[]{:S(2)}) collective-permute-start(bf16[2,256,1024]{2,1,0:T(8,128)(2,1)} %collective-permute-done.27.refs_5_), channel_id=1, source_target_pairs={{8,0},{12,4},{9,1},{13,5},{10,2},{14,6},{11,3},{15,7}} | collective-permute-start | bytes 3145736 | tf_op jit(solution)/shard_map/ppermute | solution.py:133
  202.7 76.5 %collective-permute-start.31 = (bf16[2,256,1024]{2,1,0:T(8,128)(2,1)}, bf16[2,256,1024]{2,1,0:T(8,128)(2,1)S(1)}, u32[]{:S(2)}, u32[]{:S(2)}) collective-permute-start(bf16[2,256,1024]{2,1,0:T(8,128)(2,1)} %copy-done.10), channel_id=1, source_target_pairs={{16,20},{20,16},{24,28},{28,24},{17,21},{21,17},{25,29},{29,25},{1... | collective-permute-start | bytes 3145736 | tf_op jit(solution)/shard_map/ppermute | solution.py:133
  212.8 67.2 %collective-permute-start.25 = (bf16[2,256,1024]{2,1,0:T(8,128)(2,1)}, bf16[2,256,1024]{2,1,0:T(8,128)(2,1)S(1)}, u32[]{:S(2)}, u32[]{:S(2)}) collective-permute-start(bf16[2,256,1024]{2,1,0:T(8,128)(2,1)} %copy-done.10), channel_id=1, source_target_pairs={{16,24},{20,28},{17,25},{21,29},{18,26},{22,30},{19,27},{23,31}} | collective-permute-start | bytes 3145736 | tf_op jit(solution)/shard_map/ppermute | solution.py:133
  236.9 44.7 %collective-permute-start.14 = (bf16[2,256,1024]{2,1,0:T(8,128)(2,1)}, bf16[2,256,1024]{2,1,0:T(8,128)(2,1)S(1)}, u32[]{:S(2)}, u32[]{:S(2)}) collective-permute-start(bf16[2,256,1024]{2,1,0:T(8,128)(2,1)} %collective-permute-done.7.refs_4_), channel_id=1, source_target_pairs={{0,4},{4,0},{8,12},{12,8},{16,20},{20,16},{1,5},{5,1},{9,13},{13,9... | collective-permute-start | bytes 3145736 | tf_op jit(solution)/shard_map/ppermute | solution.py:133
  277.9 18.0 %copy-start.11 = (bf16[2,256,1024]{2,1,0:T(8,128)(2,1)}, bf16[2,256,1024]{2,1,0:T(8,128)(2,1)S(1)}, u32[]{:S(2)}) copy-start(bf16[2,256,1024]{2,1,0:T(8,128)(2,1)S(1)} %collective-permute-done.28.refs_6_) | copy-start | bytes 3145732
  277.9 18.0 %collective-permute-start.8 = (bf16[2,256,1024]{2,1,0:T(8,128)(2,1)}, bf16[2,256,1024]{2,1,0:T(8,128)(2,1)}, u32[]{:S(2)}, u32[]{:S(2)}) collective-permute-start(bf16[2,256,1024]{2,1,0:T(8,128)(2,1)} %collective-permute-done.7.refs_4_), channel_id=1, source_target_pairs={{8,0},{12,4},{16,8},{20,12},{9,1},{13,5},{17,9},{21,13},{10,2},{14... | collective-permute-start | bytes 3145736 | tf_op jit(solution)/shard_map/ppermute | solution.py:133
  279.2 44.6 %copy-start.12 = (bf16[2,256,1024]{2,1,0:T(8,128)(2,1)}, bf16[2,256,1024]{2,1,0:T(8,128)(2,1)S(1)}, u32[]{:S(2)}) copy-start(bf16[2,256,1024]{2,1,0:T(8,128)(2,1)S(1)} %collective-permute-done.31.refs_9_) | copy-start | bytes 3145732
  279.2 20.0 %collective-permute-start.11 = (bf16[2,256,1024]{2,1,0:T(8,128)(2,1)}, bf16[2,256,1024]{2,1,0:T(8,128)(2,1)S(1)}, u32[]{:S(2)}, u32[]{:S(2)}) collective-permute-start(bf16[2,256,1024]{2,1,0:T(8,128)(2,1)} %collective-permute-done.4.refs_1_), channel_id=1, source_target_pairs={{8,12},{12,8},{16,20},{20,16},{24,28},{28,24},{9,13},{13,9},{17,21... | collective-permute-start | bytes 3145736 | tf_op jit(solution)/shard_map/ppermute | solution.py:133
  280.0 45.1 %copy-start.14 = (bf16[2,256,1024]{2,1,0:T(8,128)(2,1)}, bf16[2,256,1024]{2,1,0:T(8,128)(2,1)S(1)}, u32[]{:S(2)}) copy-start(bf16[2,256,1024]{2,1,0:T(8,128)(2,1)S(1)} %collective-permute-done.25.refs_3_) | copy-start | bytes 3145732
  280.0 83.2 %collective-permute-start.38 = (bf16[2048,1024]{1,0:T(8,128)(2,1)}, bf16[2048,1024]{1,0:T(8,128)(2,1)}, u32[]{:S(2)}, u32[]{:S(2)}) collective-permute-start(bf16[2048,1024]{1,0:T(8,128)(2,1)} %bitcast.17.refs_0_), channel_id=1, source_target_pairs={{0,2},{1,3},{2,0},{3,1},{4,6},{5,7},{6,4},{7,5},{8,10},{9,11},{10,... | collective-permute-start | bytes 12582920 | tf_op jit(solution)/shard_map/ppermute | solution.py:23
  281.6 43.5 %copy-start.13 = (bf16[2,256,1024]{2,1,0:T(8,128)(2,1)}, bf16[2,256,1024]{2,1,0:T(8,128)(2,1)S(1)}, u32[]{:S(2)}) copy-start(bf16[2,256,1024]{2,1,0:T(8,128)(2,1)S(1)} %collective-permute-done.14.refs_11_) | copy-start | bytes 3145732
  281.6 18.4 %collective-permute-start.5 = (bf16[2,256,1024]{2,1,0:T(8,128)(2,1)}, bf16[2,256,1024]{2,1,0:T(8,128)(2,1)}, u32[]{:S(2)}, u32[]{:S(2)}) collective-permute-start(bf16[2,256,1024]{2,1,0:T(8,128)(2,1)} %collective-permute-done.4.refs_1_), channel_id=1, source_target_pairs={{8,16},{12,20},{16,24},{20,28},{9,17},{13,21},{17,25},{21,29},{10,... | collective-permute-start | bytes 3145736 | tf_op jit(solution)/shard_map/ppermute | solution.py:133
  295.9 27.9 %collective-permute-start.35 = (bf16[2,256,1024]{2,1,0:T(8,128)(2,1)S(1)}, bf16[2,256,1024]{2,1,0:T(8,128)(2,1)S(1)}, u32[]{:S(2)}, u32[]{:S(2)}) collective-permute-start(bf16[2,256,1024]{2,1,0:T(8,128)(2,1)S(1)} %collective-permute-done.28.refs_6_), channel_id=1, source_target_pairs={{0,4},{4,0},{1,5},{5,1},{2,6},{6,2},{3,7},{7,3}} | collective-permute-start | bytes 3145736 | tf_op jit(solution)/shard_map/ppermute | solution.py:133
  299.3 27.6 %copy-start.15 = (bf16[2,256,1024]{2,1,0:T(8,128)(2,1)}, bf16[2,256,1024]{2,1,0:T(8,128)(2,1)S(1)}, u32[]{:S(2)}) copy-start(bf16[2,256,1024]{2,1,0:T(8,128)(2,1)S(1)} %collective-permute-done.11.refs_8_) | copy-start | bytes 3145732
  299.3 25.9 %collective-permute-start.32 = (bf16[2,256,1024]{2,1,0:T(8,128)(2,1)S(1)}, bf16[2,256,1024]{2,1,0:T(8,128)(2,1)S(1)}, u32[]{:S(2)}, u32[]{:S(2)}) collective-permute-start(bf16[2,256,1024]{2,1,0:T(8,128)(2,1)S(1)} %collective-permute-done.25.refs_3_), channel_id=1, source_target_pairs={{24,28},{28,24},{25,29},{29,25},{26,30},{30,26},{27,31},{31,27}} | collective-permute-start | bytes 3145736 | tf_op jit(solution)/shard_map/ppermute | solution.py:133
  300.0 36.8 %collective-permute-start.15 = (bf16[2,256,1024]{2,1,0:T(8,128)(2,1)}, bf16[2,256,1024]{2,1,0:T(8,128)(2,1)S(1)}, u32[]{:S(2)}, u32[]{:S(2)}) collective-permute-start(bf16[2,256,1024]{2,1,0:T(8,128)(2,1)} %collective-permute-done.8.refs_5_), channel_id=1, source_target_pairs={{0,4},{4,0},{8,12},{12,8},{1,5},{5,1},{9,13},{13,9},{2,6},{6,2},{1... | collective-permute-start | bytes 3145736 | tf_op jit(solution)/shard_map/ppermute | solution.py:133
  323.8 13.0 %copy-start.16 = (bf16[2,256,1024]{2,1,0:T(8,128)(2,1)}, bf16[2,256,1024]{2,1,0:T(8,128)(2,1)S(1)}, u32[]{:S(2)}) copy-start(bf16[2,256,1024]{2,1,0:T(8,128)(2,1)S(1)} %collective-permute-done.35.refs_13_) | copy-start | bytes 3145732
  323.8 21.1 %collective-permute-start.9 = (bf16[2,256,1024]{2,1,0:T(8,128)(2,1)}, bf16[2,256,1024]{2,1,0:T(8,128)(2,1)}, u32[]{:S(2)}, u32[]{:S(2)}) collective-permute-start(bf16[2,256,1024]{2,1,0:T(8,128)(2,1)} %collective-permute-done.8.refs_5_), channel_id=1, source_target_pairs={{8,0},{12,4},{9,1},{13,5},{10,2},{14,6},{11,3},{15,7}} | collective-permute-start | bytes 3145736 | tf_op jit(solution)/shard_map/ppermute | solution.py:133
  325.2 11.6 %copy-start.18 = (bf16[2,256,1024]{2,1,0:T(8,128)(2,1)}, bf16[2,256,1024]{2,1,0:T(8,128)(2,1)S(1)}, u32[]{:S(2)}) copy-start(bf16[2,256,1024]{2,1,0:T(8,128)(2,1)S(1)} %collective-permute-done.32.refs_10_) | copy-start | bytes 3145732
  325.2 23.4 %collective-permute-start.6 = (bf16[2,256,1024]{2,1,0:T(8,128)(2,1)}, bf16[2,256,1024]{2,1,0:T(8,128)(2,1)}, u32[]{:S(2)}, u32[]{:S(2)}) collective-permute-start(bf16[2,256,1024]{2,1,0:T(8,128)(2,1)} %collective-permute-done.5.refs_2_), channel_id=1, source_target_pairs={{16,24},{20,28},{17,25},{21,29},{18,26},{22,30},{19,27},{23,31}} | collective-permute-start | bytes 3145736 | tf_op jit(solution)/shard_map/ppermute | solution.py:133
  336.8 1.0 copy-start.17
  337.8 12.7 %collective-permute-start.12 = (bf16[2,256,1024]{2,1,0:T(8,128)(2,1)}, bf16[2,256,1024]{2,1,0:T(8,128)(2,1)}, u32[]{:S(2)}, u32[]{:S(2)}) collective-permute-start(bf16[2,256,1024]{2,1,0:T(8,128)(2,1)} %collective-permute-done.5.refs_2_), channel_id=1, source_target_pairs={{16,20},{20,16},{24,28},{28,24},{17,21},{21,17},{25,29},{29,25},{1... | collective-permute-start | bytes 3145736 | tf_op jit(solution)/shard_map/ppermute | solution.py:133
  344.9 18.3 %collective-permute-start.16 = (bf16[2,256,1024]{2,1,0:T(8,128)(2,1)}, bf16[2,256,1024]{2,1,0:T(8,128)(2,1)}, u32[]{:S(2)}, u32[]{:S(2)}) collective-permute-start(bf16[2,256,1024]{2,1,0:T(8,128)(2,1)} %collective-permute-done.9.refs_6_), channel_id=1, source_target_pairs={{0,4},{4,0},{1,5},{5,1},{2,6},{6,2},{3,7},{7,3}} | collective-permute-start | bytes 3145736 | tf_op jit(solution)/shard_map/ppermute | solution.py:133
  348.6 15.2 %collective-permute-start.13 = (bf16[2,256,1024]{2,1,0:T(8,128)(2,1)}, bf16[2,256,1024]{2,1,0:T(8,128)(2,1)}, u32[]{:S(2)}, u32[]{:S(2)}) collective-permute-start(bf16[2,256,1024]{2,1,0:T(8,128)(2,1)} %collective-permute-done.6.refs_3_), channel_id=1, source_target_pairs={{24,28},{28,24},{25,29},{29,25},{26,30},{30,26},{27,31},{31,27}} | collective-permute-start | bytes 3145736 | tf_op jit(solution)/shard_map/ppermute | solution.py:133
  350.5 83.4 %collective-permute-start.40 = (bf16[2048,1024]{1,0:T(8,128)(2,1)}, bf16[2048,1024]{1,0:T(8,128)(2,1)}, u32[]{:S(2)}, u32[]{:S(2)}) collective-permute-start(bf16[2048,1024]{1,0:T(8,128)(2,1)} %bitcast.17.refs_0_), channel_id=1, source_target_pairs={{0,1},{1,0},{2,3},{3,2},{4,5},{5,4},{6,7},{7,6},{8,9},{9,8},{10,11... | collective-permute-start | bytes 12582920 | tf_op jit(solution)/shard_map/ppermute | solution.py:23
  350.6 64.6 %collective-permute-start.37 = (bf16[1024,1792]{1,0:T(8,128)(2,1)}, bf16[1024,1792]{1,0:T(8,128)(2,1)}, u32[]{:S(2)}, u32[]{:S(2)}) collective-permute-start(bf16[1024,1792]{1,0:T(8,128)(2,1)} %dynamic-slice_bitcast_fusion.1), channel_id=1, source_target_pairs={{0,1},{1,0},{2,3},{3,2},{4,5},{5,4},{6,7},{7,6},{8,9},{9,8},{10,11... | collective-permute-start | bytes 11010056 | tf_op jit(solution)/shard_map/ppermute | solution.py:23
  363.2 99.3 %collective-permute-start.20 = (bf16[1024,1792]{1,0:T(8,128)(2,1)}, bf16[1024,1792]{1,0:T(8,128)(2,1)}, u32[]{:S(2)}, u32[]{:S(2)}) collective-permute-start(bf16[1024,1792]{1,0:T(8,128)(2,1)} %constant_dynamic-slice_fusion.2), channel_id=1, source_target_pairs={{0,1},{1,0},{2,3},{3,2},{4,5},{5,4},{6,7},{7,6},{8,9},{9,8},{10,11... | collective-permute-start | bytes 11010056 | tf_op jit(solution)/shard_map/ppermute | solution.py:23
  363.2 99.3 %collective-permute-start.39 = (bf16[2048,1024]{1,0:T(8,128)(2,1)}, bf16[2048,1024]{1,0:T(8,128)(2,1)}, u32[]{:S(2)}, u32[]{:S(2)}) collective-permute-start(bf16[2048,1024]{1,0:T(8,128)(2,1)} %collective-permute-done.38.refs_0_), channel_id=1, source_target_pairs={{0,1},{1,0},{2,3},{3,2},{4,5},{5,4},{6,7},{7,6},{8,9},{9,8},{10,11... | collective-permute-start | bytes 12582920 | tf_op jit(solution)/shard_map/ppermute | solution.py:23
  363.7 51.5 %copy-start.1 = (bf16[8,256,768]{2,1,0:T(8,128)(2,1)}, bf16[8,256,768]{2,1,0:T(8,128)(2,1)S(1)}, u32[]{:S(2)}) copy-start(bf16[8,256,768]{2,1,0:T(8,128)(2,1)S(1)} %all-to-all-done.1) | copy-start | bytes 9437188
  363.7 70.2 %collective-permute-start.17 = (bf16[2048,768]{1,0:T(8,128)(2,1)S(1)}, bf16[2048,768]{1,0:T(8,128)(2,1)}, u32[]{:S(2)}, u32[]{:S(2)}) collective-permute-start(bf16[2048,768]{1,0:T(8,128)(2,1)S(1)} %bitcast.61), channel_id=1, source_target_pairs={{0,2},{1,3},{2,0},{3,1},{4,6},{5,7},{6,4},{7,5},{8,10},{9,11},{10,... | collective-permute-start | bytes 9437192 | tf_op jit(solution)/shard_map/ppermute | solution.py:23
  415.3 76.9 %collective-permute-start.36 = (bf16[2048,768]{1,0:T(8,128)(2,1)S(1)}, bf16[2048,768]{1,0:T(8,128)(2,1)}, u32[]{:S(2)}, u32[]{:S(2)}) collective-permute-start(bf16[2048,768]{1,0:T(8,128)(2,1)S(1)} %bitcast.62), channel_id=1, source_target_pairs={{0,1},{1,0},{2,3},{3,2},{4,5},{5,4},{6,7},{7,6},{8,9},{9,8},{10,11... | collective-permute-start | bytes 9437192 | tf_op jit(solution)/shard_map/ppermute | solution.py:23
  433.9 81.5 %collective-permute-start.18 = (bf16[2048,768]{1,0:T(8,128)(2,1)}, bf16[2048,768]{1,0:T(8,128)(2,1)}, u32[]{:S(2)}, u32[]{:S(2)}) collective-permute-start(bf16[2048,768]{1,0:T(8,128)(2,1)} %collective-permute-done.17.refs_0_), channel_id=1, source_target_pairs={{0,1},{1,0},{2,3},{3,2},{4,5},{5,4},{6,7},{7,6},{8,9},{9,8},{10,11... | collective-permute-start | bytes 9437192 | tf_op jit(solution)/shard_map/ppermute | solution.py:23
where the time goes:
time: 550 us; the launch traced here: 540 us
  waiting for transfers between devices  231 us (42%)
  Pallas kernels  156 us (28%)
  starting transfers between devices  101 us (18%)
  local copies, waits for them, and re-layouts  46.3 us (8%)
    ppermute x26, waiting for transfers between devices, send(): return lax.ppermute(value, 'fsdp', pairs)  204 us
    pallas_call x4, Pallas kernels, add_slots(): pl.pallas_call(functools.partial(slot_kernel, slots, first, last, group_s...  106 us
    ppermute x26, starting transfers between devices, send(): return lax.ppermute(value, 'fsdp', pairs)  81.9 us
    pallas_call x2, Pallas kernels, permute_pair(): pl.pallas_call(functools.partial(permute_kernel, n), out_shape=jax.ShapeD...  49.9 us
    ppermute x15, waiting for transfers between devices, swap(): return lax.ppermute(value, axis, [(i, i ^ bit) for i in range(size)])  26.1 us
    unnamed x44, local copies, waits for them, and re-layouts  16.7 us
  transfers between devices with their start and end apart: 43, of which 14 were waited for; matrix products, arithmetic and copies ran while one was open for 7% of the time, Pallas kernels for 24%

commit v1 on v0

--- a/solution.py
+++ b/solution.py
@@ -195,7 +195,7 @@
     n = len(right)
     _, local, features = right[0].shape
     tokens = ids.shape[1]
-    rows = min(2 * ROWS, tokens)
+    rows = min(ROWS, tokens)
     me = lax.axis_index("fsdp")
     where = jnp.stack([me // 2, me % 2]).astype(jnp.int32)
     operands = [*right, *left[1:], *pair_right, *pair_left[1:]]
@@ -307,11 +307,11 @@
     bounds = jnp.stack(
         [jnp.append(m[:2 * count], jnp.int32(row)) for m, row in zip(metas, weight_rows)]
     )
-    plan = ((0, 1), (2, 3))
+    plans = ((0, 1), (2, 3)), ((0,), (1,), (2,), (3,))
     done = None
     for index, (low, high) in enumerate(chunks):
         carry = None
-        for slots in plan:
+        for slots in plans[index]:
             last = slots[-1] == size - 1
             take = lambda values: [values[j] for j in slots]
             carry = add_slots(

time: 550 us -> 584 us (1.062)
  the two profiles are of different devices: /device:TPU:0 before, /device:TPU:13 now
where the time goes in v1:
time: 584 us; the launch traced here: 575 us
  waiting for transfers between devices  254 us (43%)
  Pallas kernels  169 us (29%)
  starting transfers between devices  105 us (18%)
  local copies, waits for them, and re-layouts  43.1 us (7%)
    ppermute x26, waiting for transfers between devices, send(): return lax.ppermute(value, 'fsdp', pairs)  210 us
    pallas_call x6, Pallas kernels, add_slots(): pl.pallas_call(functools.partial(slot_kernel, slots, first, last, group_s...  114 us
    ppermute x26, starting transfers between devices, send(): return lax.ppermute(value, 'fsdp', pairs)  80.1 us
    pallas_call x2, Pallas kernels, permute_pair(): pl.pallas_call(functools.partial(permute_kernel, n), out_shape=jax.ShapeD...  54.7 us
    ppermute x15, waiting for transfers between devices, swap(): return lax.ppermute(value, axis, [(i, i ^ bit) for i in range(size)])  44.4 us
    unnamed x38, local copies, waits for them, and re-layouts  14.8 us
    ppermute x15, starting transfers between devices, swap(): return lax.ppermute(value, axis, [(i, i ^ bit) for i in range(size)])  13.2 us
    all_to_all x2, starting transfers between devices, body(): lax.all_to_all(piece, 'fsdp', split_axis=0, concat_axis=0, tiled=True)  11.8 us
  transfers between devices with their start and end apart: 43, of which 14 were waited for; matrix products, arithmetic and copies ran while one was open for 6% of the time, Pallas kernels for 27%

profile of v1, /device:TPU:13, one launch (start us, length us, event | category | flops | bytes accessed | tf_op | source)
XLA Modules:
  0.0 574.8 jit_solution(17211026027309325042)
XLA Ops:
  0.6 5.2 copy.26
  6.4 2.5 copy-done
  8.9 4.3 copy.31
  13.1 5.7 all-to-all-start
  18.8 3.3 reshape_squeeze.7
  22.2 2.2 constant_dynamic-slice_fusion.1
  26.0 1.4 collective-permute-done.22
  27.4 1.9 collective-permute-start.26
  33.2 1.7 collective-permute-start.29
  35.7 19.8 %collective-permute-done.1 = s32[2064]{0:T(1024)S(1)} collective-permute-done((s32[2064]{0:T(1024)S(1)}, s32[2064]{0:T(1024)S(1)}, u32[]{:S(2)}, u32[]{:S(2)}) %collective-permute-start.1) | collective-permute-done | bytes 8288 | tf_op jit(solution)/shard_map/ppermute | solution.py:23
  55.5 3.1 collective-permute-start.23
  58.6 6.5 %dynamic-slice_bitcast_fusion = bf16[2048,1792]{1,0:T(8,128)(2,1)} fusion(bf16[1,1,4096,1792]{3,2,1,0:T(8,128)(2,1)} %param.9, s32[]{:T(128)S(6)} %select_n.58), kind=kLoop, calls=%fused_computation | loop fusion | bytes 14680068 | tf_op jit(solution)/shard_map/dynamic_slice | solution.py:258
  65.1 67.5 %collective-permute-done.26.refs_4_ = bf16[2,256,1024]{2,1,0:T(8,128)(2,1)} collective-permute-done((bf16[2,256,1024]{2,1,0:T(8,128)(2,1)S(1)}, bf16[2,256,1024]{2,1,0:T(8,128)(2,1)}, u32[]{:S(2)}, u32[]{:S(2)}) %collective-permute-start.26) | collective-permute-done | bytes 1048608 | tf_op jit(solution)/shard_map/ppermute | solution.py:133
  132.6 3.4 collective-permute-start.33
  136.4 1.9 collective-permute-start.27
  138.4 2.0 collective-permute-start.3
  140.4 2.2 collective-permute-start.30
  142.6 15.0 %collective-permute-start.24 = (bf16[2,256,1024]{2,1,0:T(8,128)(2,1)S(1)}, bf16[2,256,1024]{2,1,0:T(8,128)(2,1)}, u32[]{:S(2)}, u32[]{:S(2)}) collective-permute-start(bf16[2,256,1024]{2,1,0:T(8,128)(2,1)S(1)} %collective-permute-done.23.refs_1_), channel_id=1, source_target_pairs={{8,16},{12,20},{16,24},{20,28},{9,17},{13,21},{17,25},{21,29},{10,... | collective-permute-start | bytes 3145736 | tf_op jit(solution)/shard_map/ppermute | solution.py:133
  157.9 1.7 collective-permute-start.10
  159.7 1.6 collective-permute-done.27.refs_5_
  161.3 2.2 collective-permute-start.7
  163.5 16.9 %collective-permute-done.30.refs_8_ = bf16[2,256,1024]{2,1,0:T(8,128)(2,1)S(1)} collective-permute-done((bf16[2,256,1024]{2,1,0:T(8,128)(2,1)S(1)}, bf16[2,256,1024]{2,1,0:T(8,128)(2,1)S(1)}, u32[]{:S(2)}, u32[]{:S(2)}) %collective-permute-start.30) | collective-permute-done | bytes 1048608 | tf_op jit(solution)/shard_map/ppermute | solution.py:133
  180.4 1.9 collective-permute-start.4
  182.3 3.6 collective-permute-start.34
  186.0 16.9 %collective-permute-done.10.refs_7_ = bf16[2,256,1024]{2,1,0:T(8,128)(2,1)S(1)} collective-permute-done((bf16[2,256,1024]{2,1,0:T(8,128)(2,1)S(1)}, bf16[2,256,1024]{2,1,0:T(8,128)(2,1)S(1)}, u32[]{:S(2)}, u32[]{:S(2)}) %collective-permute-start.10) | collective-permute-done | bytes 1048608 | tf_op jit(solution)/shard_map/ppermute | solution.py:133
  202.9 2.2 collective-permute-start.28
  205.1 1.6 collective-permute-start.31
  206.8 1.6 collective-permute-start.25
  208.4 16.9 %collective-permute-done.34.refs_12_ = bf16[2,256,1024]{2,1,0:T(8,128)(2,1)S(1)} collective-permute-done((bf16[2,256,1024]{2,1,0:T(8,128)(2,1)S(1)}, bf16[2,256,1024]{2,1,0:T(8,128)(2,1)S(1)}, u32[]{:S(2)}, u32[]{:S(2)}) %collective-permute-start.34) | collective-permute-done | bytes 1048608 | tf_op jit(solution)/shard_map/ppermute | solution.py:133
  225.3 3.6 collective-permute-start.14
  229.0 2.1 slice.41
  231.1 2.3 copy.32
  233.7 1.9 collective-permute-start.8
  235.6 1.9 collective-permute-start.11
  237.6 6.1 %all-to-all-start.1 = ((bf16[8,256,768]{2,1,0:T(8,128)(2,1)}), bf16[8,256,768]{2,1,0:T(8,128)(2,1)S(1)}, u32[]{:S(2)}, u32[]{:S(2)}) async-start(bf16[8,256,768]{2,1,0:T(8,128)(2,1)} %bitcast.52), calls=%async_computation.1 | async-start | bytes 6291456 | tf_op jit(solution)/shard_map/all_to_all | solution.py:282
  243.6 13.4 %collective-permute-done.14.refs_11_ = bf16[2,256,1024]{2,1,0:T(8,128)(2,1)} collective-permute-done((bf16[2,256,1024]{2,1,0:T(8,128)(2,1)}, bf16[2,256,1024]{2,1,0:T(8,128)(2,1)}, u32[]{:S(2)}, u32[]{:S(2)}) %collective-permute-start.14) | collective-permute-done | bytes 1048608 | tf_op jit(solution)/shard_map/ppermute | solution.py:133
  257.0 13.0 %collective-permute-start.5 = (bf16[2,256,1024]{2,1,0:T(8,128)(2,1)}, bf16[2,256,1024]{2,1,0:T(8,128)(2,1)}, u32[]{:S(2)}, u32[]{:S(2)}) collective-permute-start(bf16[2,256,1024]{2,1,0:T(8,128)(2,1)} %collective-permute-done.4.refs_1_), channel_id=1, source_target_pairs={{8,16},{12,20},{16,24},{20,28},{9,17},{13,21},{17,25},{21,29},{10,... | collective-permute-start | bytes 3145736 | tf_op jit(solution)/shard_map/ppermute | solution.py:133
  270.0 1.6 collective-permute-start.35
  271.7 19.7 %collective-permute-done.11.refs_8_ = bf16[2,256,1024]{2,1,0:T(8,128)(2,1)} collective-permute-done((bf16[2,256,1024]{2,1,0:T(8,128)(2,1)}, bf16[2,256,1024]{2,1,0:T(8,128)(2,1)}, u32[]{:S(2)}, u32[]{:S(2)}) %collective-permute-start.11) | collective-permute-done | bytes 1048608 | tf_op jit(solution)/shard_map/ppermute | solution.py:133
  291.3 1.6 collective-permute-start.32
  293.0 41.3 %collective-permute-done.5.refs_2_ = bf16[2,256,1024]{2,1,0:T(8,128)(2,1)} collective-permute-done((bf16[2,256,1024]{2,1,0:T(8,128)(2,1)}, bf16[2,256,1024]{2,1,0:T(8,128)(2,1)}, u32[]{:S(2)}, u32[]{:S(2)}) %collective-permute-start.5) | collective-permute-done | bytes 1048608 | tf_op jit(solution)/shard_map/ppermute | solution.py:133
  334.3 3.2 collective-permute-start.15
  337.5 2.3 collective-permute-start.9
  339.8 1.6 collective-permute-start.12
  341.4 4.1 dynamic-slice_bitcast_fusion.1
  345.6 15.1 %collective-permute-done.15.refs_12_ = bf16[2,256,1024]{2,1,0:T(8,128)(2,1)} collective-permute-done((bf16[2,256,1024]{2,1,0:T(8,128)(2,1)}, bf16[2,256,1024]{2,1,0:T(8,128)(2,1)}, u32[]{:S(2)}, u32[]{:S(2)}) %collective-permute-start.15) | collective-permute-done | bytes 1048608 | tf_op jit(solution)/shard_map/ppermute | solution.py:133
  360.7 1.7 collective-permute-start.6
  364.0 1.4 collective-permute-start.40
  365.6 2.0 copy.15.ids
  367.5 2.0 copy.20.ids
  370.1 1.6 collective-permute-start.16
  371.7 1.7 collective-permute-start.13
  373.4 10.8 %collective-permute-done.38.refs_0_ = bf16[2048,1024]{1,0:T(8,128)(2,1)} collective-permute-done((bf16[2048,1024]{1,0:T(8,128)(2,1)}, bf16[2048,1024]{1,0:T(8,128)(2,1)}, u32[]{:S(2)}, u32[]{:S(2)}) %collective-permute-start.38) | collective-permute-done | bytes 4194336 | tf_op jit(solution)/shard_map/ppermute | solution.py:23
  384.2 2.5 collective-permute-start.39
  386.7 27.3 %shard_map.69.act = bf16[2,1024,2048]{2,1,0:T(8,128)(2,1)} custom-call(s32[2]{0:T(128)} %pad_add_fusion.4.where, s32[2,2048,1]{2,1,0:T(8,128)} %copy.20.ids, bf16[2,256,1024]{2,1,0:T(8,128)(2,1)} %copy-done.2, bf16[2,256,1024]{2,1,0:T(8,128)(2,1)} %copy-done.10, bf16[2,256,1024]{2,1,0:T(8,128)(2,1)} %collective-permute-done.24.refs_2_, ...), custom_call_target="tpu_custom_call" | custom-call | flops 17179869184 | bytes 16777216 | tf_op jit(solution)/shard_map/pallas_call | solution.py:202
  414.1 4.1 constant_dynamic-slice_fusion.2
  418.5 27.4 %shard_map.68.act = bf16[2,1024,2048]{2,1,0:T(8,128)(2,1)} custom-call(s32[2]{0:T(128)} %pad_add_fusion.4.where, s32[2,2048,1]{2,1,0:T(8,128)} %copy.15.ids, bf16[2,256,1024]{2,1,0:T(8,128)(2,1)} %copy-done.3, bf16[2,256,1024]{2,1,0:T(8,128)(2,1)} %collective-permute-done.4.refs_1_, bf16[2,256,1024]{2,1,0:T(8,128)(2,1)} %collective-permute-done.5.refs_2_, ...), custom_call_target="tpu_custom_call" | custom-call | flops 17179869184 | bytes 16777216 | tf_op jit(solution)/shard_map/pallas_call | solution.py:202
  446.7 28.4 %shard_map.73 = (f32[1024,1024]{1,0:T(8,128)}, f32[1024,1024]{1,0:T(8,128)}) custom-call(s32[2,17]{1,0:T(2,128)} %pad_add_fusion.1.bounds, bf16[2,1024,2048]{2,1,0:T(8,128)(2,1)} %shard_map.69.act, bf16[2048,1024]{1,0:T(8,128)(2,1)} %bitcast.15.refs_0_, bf16[2048,1024]{1,0:T(8,128)(2,1)} %collective-permute-done.40.refs_1_, bf16[4096,1792]{1,0:T(8,128)(2,1)} %bitcast.55, ...), custom_call_target="tpu_custom_call" | custom-call | flops 17179869184 | bytes 35651584 | tf_op jit(solution)/shard_map/pallas_call | solution.py:106
  475.1 12.4 %collective-permute-done.17.refs_0_ = bf16[2048,768]{1,0:T(8,128)(2,1)} collective-permute-done((bf16[2048,768]{1,0:T(8,128)(2,1)S(1)}, bf16[2048,768]{1,0:T(8,128)(2,1)}, u32[]{:S(2)}, u32[]{:S(2)}) %collective-permute-start.17) | collective-permute-done | bytes 3145760 | tf_op jit(solution)/shard_map/ppermute | solution.py:23
  488.9 12.8 %shard_map.70 = (f32[1024,768]{1,0:T(8,128)}, f32[1024,768]{1,0:T(8,128)}) custom-call(s32[1,17]{1,0:T(1,128)} %copy-done.5, bf16[2,1024,2048]{2,1,0:T(8,128)(2,1)} %shard_map.69.act, bf16[2048,768]{1,0:T(8,128)(2,1)} %bitcast.62, bf16[4096,1792]{1,0:T(8,128)(2,1)} %bitcast.56), custom_call_target="tpu_custom_call" | custom-call | flops 6442450944 | bytes 21495808 | tf_op jit(solution)/shard_map/pallas_call | solution.py:106
  501.7 30.1 %shard_map.74 = (bf16[1024,1792]{1,0:T(8,128)(2,1)}, f32[1024,1792]{1,0:T(8,128)}) custom-call(s32[2,17]{1,0:T(2,128)} %pad_add_fusion.bounds, bf16[2,1024,2048]{2,1,0:T(8,128)(2,1)} %shard_map.68.act, bf16[2048,1024]{1,0:T(8,128)(2,1)} %collective-permute-done.38.refs_0_, bf16[2048,1024]{1,0:T(8,128)(2,1)} %collective-permute-done.39.refs_1_, ...), custom_call_target="tpu_custom_call" | custom-call | flops 17179869184 | bytes 35651584 | tf_op jit(solution)/shard_map/pallas_call | solution.py:106
  531.8 13.9 %shard_map.71 = (f32[1024,768]{1,0:T(8,128)}, f32[1024,768]{1,0:T(8,128)}) custom-call(s32[1,17]{1,0:T(1,128)} %copy-done.9, bf16[2,1024,2048]{2,1,0:T(8,128)(2,1)} %shard_map.69.act, bf16[2048,768]{1,0:T(8,128)(2,1)} %collective-permute-done.36.refs_0_, bf16[1024,1792]{1,0:T(8,128)(2,1)} %collective-permute-done.37.refs_1_.refs_3_, ...), custom_call_target="tpu_custom_call" | custom-call | flops 6442450944 | bytes 21495808 | tf_op jit(solution)/shard_map/pallas_call | solution.py:106
  545.7 14.2 %shard_map.72 = (f32[1024,768]{1,0:T(8,128)}, f32[1024,768]{1,0:T(8,128)}) custom-call(s32[1,17]{1,0:T(1,128)} %copy-done.7, bf16[2,1024,2048]{2,1,0:T(8,128)(2,1)} %shard_map.68.act, bf16[2048,768]{1,0:T(8,128)(2,1)} %collective-permute-done.17.refs_0_, bf16[2048,1792]{1,0:T(8,128)(2,1)} %collective-permute-done.19.refs_1_.refs_2_, ...), custom_call_target="tpu_custom_call" | custom-call | flops 6442450944 | bytes 21495808 | tf_op jit(solution)/shard_map/pallas_call | solution.py:106
  559.9 14.4 %shard_map.75 = (bf16[1024,1792]{1,0:T(8,128)(2,1)}, f32[1024,1792]{1,0:T(8,128)}) custom-call(s32[1,17]{1,0:T(1,128)} %copy-done.6, bf16[2,1024,2048]{2,1,0:T(8,128)(2,1)} %shard_map.68.act, bf16[2048,768]{1,0:T(8,128)(2,1)} %collective-permute-done.18.refs_0_, ...), custom_call_target="tpu_custom_call", output_to_operand_aliasing={{0}: (6, {}), {1}: (7, {})} | custom-call | flops 6442450944 | bytes 21495808 | tf_op jit(solution)/shard_map/pallas_call | solution.py:106
  (99 shorter events, 12.8 us)
Async XLA Ops:
  5.8 3.1 copy-start
  13.1 220.3 %all-to-all-start = ((bf16[8,256,1024]{2,1,0:T(8,128)(2,1)}), bf16[8,256,1024]{2,1,0:T(8,128)(2,1)}, u32[]{:S(2)}, u32[]{:S(2)}) async-start(bf16[8,256,1024]{2,1,0:T(8,128)(2,1)} %bitcast.59), calls=%async_computation | async-start | bytes 8388608 | tf_op jit(solution)/shard_map/all_to_all | solution.py:282
  24.5 2.8 collective-permute-start.22
  25.8 5.2 copy-start.8
  25.8 5.4 copy-start.4
  27.4 37.6 %copy-start.2 = (bf16[2,256,1024]{2,1,0:T(8,128)(2,1)}, bf16[2,256,1024]{2,1,0:T(8,128)(2,1)S(1)}, u32[]{:S(2)}) copy-start(bf16[2,256,1024]{2,1,0:T(8,128)(2,1)S(1)} %pad_maximum_fusion.1.refs_0_) | copy-start | bytes 3145732
  27.4 105.1 %collective-permute-start.26 = (bf16[2,256,1024]{2,1,0:T(8,128)(2,1)S(1)}, bf16[2,256,1024]{2,1,0:T(8,128)(2,1)}, u32[]{:S(2)}, u32[]{:S(2)}) collective-permute-start(bf16[2,256,1024]{2,1,0:T(8,128)(2,1)S(1)} %pad_maximum_fusion.1.refs_0_), channel_id=1, source_target_pairs={{8,0},{12,4},{16,8},{20,12},{24,16},{28,20},{9,1},{13,5},{17,9},{2... | collective-permute-start | bytes 3145736 | tf_op jit(solution)/shard_map/ppermute | solution.py:133
  30.8 105.6 %collective-permute-start.2 = (bf16[256,1,2,1024]{3,0,2,1:T(8,128)(2,1)S(1)}, bf16[256,1,2,1024]{3,0,2,1:T(8,128)(2,1)S(1)}, u32[]{:S(2)}, u32[]{:S(2)}) collective-permute-start(bf16[256,1,2,1024]{3,0,2,1:T(8,128)(2,1)S(1)} %copy.21), channel_id=1, source_target_pairs={{0,2},{1,3},{2,0},{3,1},{4,6},{5,7},{6,4},{7,5},{8,10},{9,11},{10,... | collective-permute-start | bytes 3145736 | tf_op jit(solution)/shard_map/ppermute | solution.py:23
  31.3 3.6 collective-permute-start.21
  32.0 23.6 %collective-permute-start.1 = (s32[2064]{0:T(1024)S(1)}, s32[2064]{0:T(1024)S(1)}, u32[]{:S(2)}, u32[]{:S(2)}) collective-permute-start(s32[2064]{0:T(1024)S(1)} %concatenate.20), channel_id=1, source_target_pairs={{0,2},{1,3},{2,0},{3,1},{4,6},{5,7},{6,4},{7,5},{8,10},{9,11},{10,... | collective-permute-start | bytes 24776 | tf_op jit(solution)/shard_map/ppermute | solution.py:23
  33.2 105.1 %collective-permute-start.29 = (bf16[2,256,1024]{2,1,0:T(8,128)(2,1)S(1)}, bf16[2,256,1024]{2,1,0:T(8,128)(2,1)}, u32[]{:S(2)}, u32[]{:S(2)}) collective-permute-start(bf16[2,256,1024]{2,1,0:T(8,128)(2,1)S(1)} %pad_maximum_fusion.1.refs_0_), channel_id=1, source_target_pairs={{0,4},{4,0},{8,12},{12,8},{16,20},{20,16},{24,28},{28,24},{1,5},{5... | collective-permute-start | bytes 3145736 | tf_op jit(solution)/shard_map/ppermute | solution.py:133
  35.0 101.1 %collective-permute-start = (s32[2064]{0:T(1024)S(1)}, s32[2064]{0:T(1024)S(1)}, u32[]{:S(2)}, u32[]{:S(2)}) collective-permute-start(s32[2064]{0:T(1024)S(1)} %concatenate.20), channel_id=1, source_target_pairs={{0,3},{1,2},{2,1},{3,0},{4,7},{5,6},{6,5},{7,4},{8,11},{9,10},{10,... | collective-permute-start | bytes 24776 | tf_op jit(solution)/shard_map/ppermute | solution.py:23
  55.5 84.9 %collective-permute-start.23 = (bf16[2,256,1024]{2,1,0:T(8,128)(2,1)S(1)}, bf16[2,256,1024]{2,1,0:T(8,128)(2,1)S(1)}, u32[]{:S(2)}, u32[]{:S(2)}) collective-permute-start(bf16[2,256,1024]{2,1,0:T(8,128)(2,1)S(1)} %pad_maximum_fusion.1.refs_0_), channel_id=1, source_target_pairs={{0,8},{4,12},{8,16},{12,20},{16,24},{20,28},{1,9},{5,13},{9,17},{1... | collective-permute-start | bytes 3145736 | tf_op jit(solution)/shard_map/ppermute | solution.py:133
  132.6 25.3 %collective-permute-start.33 = (bf16[2,256,1024]{2,1,0:T(8,128)(2,1)}, bf16[2,256,1024]{2,1,0:T(8,128)(2,1)S(1)}, u32[]{:S(2)}, u32[]{:S(2)}) collective-permute-start(bf16[2,256,1024]{2,1,0:T(8,128)(2,1)} %collective-permute-done.26.refs_4_), channel_id=1, source_target_pairs={{0,4},{4,0},{8,12},{12,8},{16,20},{20,16},{1,5},{5,1},{9,13},{13,9... | collective-permute-start | bytes 3145736 | tf_op jit(solution)/shard_map/ppermute | solution.py:133
  136.1 235.7 %collective-permute-start.19 = (bf16[2048,1792]{1,0:T(8,128)(2,1)}, bf16[2048,1792]{1,0:T(8,128)(2,1)}, u32[]{:S(2)}, u32[]{:S(2)}) collective-permute-start(bf16[2048,1792]{1,0:T(8,128)(2,1)} %dynamic-slice_bitcast_fusion), channel_id=1, source_target_pairs={{0,2},{1,3},{2,0},{3,1},{4,6},{5,7},{6,4},{7,5},{8,10},{9,11},{10,... | collective-permute-start | bytes 22020104 | tf_op jit(solution)/shard_map/ppermute | solution.py:23
  136.4 25.0 %collective-permute-start.27 = (bf16[2,256,1024]{2,1,0:T(8,128)(2,1)}, bf16[2,256,1024]{2,1,0:T(8,128)(2,1)S(1)}, u32[]{:S(2)}, u32[]{:S(2)}) collective-permute-start(bf16[2,256,1024]{2,1,0:T(8,128)(2,1)} %collective-permute-done.26.refs_4_), channel_id=1, source_target_pairs={{8,0},{12,4},{16,8},{20,12},{9,1},{13,5},{17,9},{21,13},{10,2},{14... | collective-permute-start | bytes 3145736 | tf_op jit(solution)/shard_map/ppermute | solution.py:133
  138.4 4.2 collective-permute-start.3
  140.4 90.7 %copy-start.10 = (bf16[2,256,1024]{2,1,0:T(8,128)(2,1)}, bf16[2,256,1024]{2,1,0:T(8,128)(2,1)S(1)}, u32[]{:S(2)}) copy-start(bf16[2,256,1024]{2,1,0:T(8,128)(2,1)S(1)} %collective-permute-done.23.refs_1_) | copy-start | bytes 3145732
  140.4 40.0 %collective-permute-start.30 = (bf16[2,256,1024]{2,1,0:T(8,128)(2,1)S(1)}, bf16[2,256,1024]{2,1,0:T(8,128)(2,1)S(1)}, u32[]{:S(2)}, u32[]{:S(2)}) collective-permute-start(bf16[2,256,1024]{2,1,0:T(8,128)(2,1)S(1)} %collective-permute-done.23.refs_1_), channel_id=1, source_target_pairs={{8,12},{12,8},{16,20},{20,16},{24,28},{28,24},{9,13},{13,9},{17,21... | collective-permute-start | bytes 3145736 | tf_op jit(solution)/shard_map/ppermute | solution.py:133
  142.6 39.7 %collective-permute-start.24 = (bf16[2,256,1024]{2,1,0:T(8,128)(2,1)S(1)}, bf16[2,256,1024]{2,1,0:T(8,128)(2,1)}, u32[]{:S(2)}, u32[]{:S(2)}) collective-permute-start(bf16[2,256,1024]{2,1,0:T(8,128)(2,1)S(1)} %collective-permute-done.23.refs_1_), channel_id=1, source_target_pairs={{8,16},{12,20},{16,24},{20,28},{9,17},{13,21},{17,25},{21,29},{10,... | collective-permute-start | bytes 3145736 | tf_op jit(solution)/shard_map/ppermute | solution.py:133
  157.7 67.6 %copy-start.3 = (bf16[2,256,1024]{2,1,0:T(8,128)(2,1)}, bf16[2,256,1024]{2,1,0:T(8,128)(2,1)S(1)}, u32[]{:S(2)}) copy-start(bf16[2,256,1024]{2,1,0:T(8,128)(2,1)S(1)} %pad_maximum_fusion.refs_0_) | copy-start | bytes 3145732
  157.9 71.1 %copy-start.11 = (bf16[2,256,1024]{2,1,0:T(8,128)(2,1)}, bf16[2,256,1024]{2,1,0:T(8,128)(2,1)S(1)}, u32[]{:S(2)}) copy-start(bf16[2,256,1024]{2,1,0:T(8,128)(2,1)S(1)} %collective-permute-done.33.refs_11_) | copy-start | bytes 3145732
  157.9 44.9 %collective-permute-start.10 = (bf16[2,256,1024]{2,1,0:T(8,128)(2,1)S(1)}, bf16[2,256,1024]{2,1,0:T(8,128)(2,1)S(1)}, u32[]{:S(2)}, u32[]{:S(2)}) collective-permute-start(bf16[2,256,1024]{2,1,0:T(8,128)(2,1)S(1)} %pad_maximum_fusion.refs_0_), channel_id=1, source_target_pairs={{0,4},{4,0},{8,12},{12,8},{16,20},{20,16},{24,28},{28,24},{1,5},{5... | collective-permute-start | bytes 3145736 | tf_op jit(solution)/shard_map/ppermute | solution.py:133
  161.3 72.1 %copy-start.12 = (bf16[2,256,1024]{2,1,0:T(8,128)(2,1)}, bf16[2,256,1024]{2,1,0:T(8,128)(2,1)S(1)}, u32[]{:S(2)}) copy-start(bf16[2,256,1024]{2,1,0:T(8,128)(2,1)S(1)} %collective-permute-done.27.refs_5_) | copy-start | bytes 3145732
  161.3 43.8 %collective-permute-start.7 = (bf16[2,256,1024]{2,1,0:T(8,128)(2,1)S(1)}, bf16[2,256,1024]{2,1,0:T(8,128)(2,1)}, u32[]{:S(2)}, u32[]{:S(2)}) collective-permute-start(bf16[2,256,1024]{2,1,0:T(8,128)(2,1)S(1)} %pad_maximum_fusion.refs_0_), channel_id=1, source_target_pairs={{8,0},{12,4},{16,8},{20,12},{24,16},{28,20},{9,1},{13,5},{17,9},{2... | collective-permute-start | bytes 3145736 | tf_op jit(solution)/shard_map/ppermute | solution.py:133
  180.4 53.0 %copy-start.14 = (bf16[2,256,1024]{2,1,0:T(8,128)(2,1)}, bf16[2,256,1024]{2,1,0:T(8,128)(2,1)S(1)}, u32[]{:S(2)}) copy-start(bf16[2,256,1024]{2,1,0:T(8,128)(2,1)S(1)} %collective-permute-done.30.refs_8_) | copy-start | bytes 3145732
  180.4 26.4 %collective-permute-start.4 = (bf16[2,256,1024]{2,1,0:T(8,128)(2,1)S(1)}, bf16[2,256,1024]{2,1,0:T(8,128)(2,1)}, u32[]{:S(2)}, u32[]{:S(2)}) collective-permute-start(bf16[2,256,1024]{2,1,0:T(8,128)(2,1)S(1)} %pad_maximum_fusion.refs_0_), channel_id=1, source_target_pairs={{0,8},{4,12},{8,16},{12,20},{16,24},{20,28},{1,9},{5,13},{9,17},{1... | collective-permute-start | bytes 3145736 | tf_op jit(solution)/shard_map/ppermute | solution.py:133
  182.3 43.0 %collective-permute-start.34 = (bf16[2,256,1024]{2,1,0:T(8,128)(2,1)S(1)}, bf16[2,256,1024]{2,1,0:T(8,128)(2,1)S(1)}, u32[]{:S(2)}, u32[]{:S(2)}) collective-permute-start(bf16[2,256,1024]{2,1,0:T(8,128)(2,1)S(1)} %collective-permute-done.27.refs_5_), channel_id=1, source_target_pairs={{0,4},{4,0},{8,12},{12,8},{1,5},{5,1},{9,13},{13,9},{2,6},{6,2},{1... | collective-permute-start | bytes 3145736 | tf_op jit(solution)/shard_map/ppermute | solution.py:133
  202.9 30.5 %copy-start.13 = (bf16[2,256,1024]{2,1,0:T(8,128)(2,1)}, bf16[2,256,1024]{2,1,0:T(8,128)(2,1)S(1)}, u32[]{:S(2)}) copy-start(bf16[2,256,1024]{2,1,0:T(8,128)(2,1)S(1)} %collective-permute-done.10.refs_7_) | copy-start | bytes 3145732
  202.9 30.5 %collective-permute-start.28 = (bf16[2,256,1024]{2,1,0:T(8,128)(2,1)S(1)}, bf16[2,256,1024]{2,1,0:T(8,128)(2,1)}, u32[]{:S(2)}, u32[]{:S(2)}) collective-permute-start(bf16[2,256,1024]{2,1,0:T(8,128)(2,1)S(1)} %collective-permute-done.27.refs_5_), channel_id=1, source_target_pairs={{8,0},{12,4},{9,1},{13,5},{10,2},{14,6},{11,3},{15,7}} | collective-permute-start | bytes 3145736 | tf_op jit(solution)/shard_map/ppermute | solution.py:133
  205.1 28.6 %collective-permute-start.31 = (bf16[2,256,1024]{2,1,0:T(8,128)(2,1)}, bf16[2,256,1024]{2,1,0:T(8,128)(2,1)}, u32[]{:S(2)}, u32[]{:S(2)}) collective-permute-start(bf16[2,256,1024]{2,1,0:T(8,128)(2,1)} %collective-permute-done.24.refs_2_), channel_id=1, source_target_pairs={{16,20},{20,16},{24,28},{28,24},{17,21},{21,17},{25,29},{29,25},{1... | collective-permute-start | bytes 3145736 | tf_op jit(solution)/shard_map/ppermute | solution.py:133
  206.8 28.9 %collective-permute-start.25 = (bf16[2,256,1024]{2,1,0:T(8,128)(2,1)}, bf16[2,256,1024]{2,1,0:T(8,128)(2,1)}, u32[]{:S(2)}, u32[]{:S(2)}) collective-permute-start(bf16[2,256,1024]{2,1,0:T(8,128)(2,1)} %collective-permute-done.24.refs_2_), channel_id=1, source_target_pairs={{16,24},{20,28},{17,25},{21,29},{18,26},{22,30},{19,27},{23,31}} | collective-permute-start | bytes 3145736 | tf_op jit(solution)/shard_map/ppermute | solution.py:133
  225.3 5.8 %copy-start.15 = (bf16[2,256,1024]{2,1,0:T(8,128)(2,1)}, bf16[2,256,1024]{2,1,0:T(8,128)(2,1)S(1)}, u32[]{:S(2)}) copy-start(bf16[2,256,1024]{2,1,0:T(8,128)(2,1)S(1)} %collective-permute-done.34.refs_12_) | copy-start | bytes 3145732
  225.3 31.7 %collective-permute-start.14 = (bf16[2,256,1024]{2,1,0:T(8,128)(2,1)}, bf16[2,256,1024]{2,1,0:T(8,128)(2,1)}, u32[]{:S(2)}, u32[]{:S(2)}) collective-permute-start(bf16[2,256,1024]{2,1,0:T(8,128)(2,1)} %collective-permute-done.7.refs_4_), channel_id=1, source_target_pairs={{0,4},{4,0},{8,12},{12,8},{16,20},{20,16},{1,5},{5,1},{9,13},{13,9... | collective-permute-start | bytes 3145736 | tf_op jit(solution)/shard_map/ppermute | solution.py:133
  233.4 150.8 %collective-permute-start.38 = (bf16[2048,1024]{1,0:T(8,128)(2,1)}, bf16[2048,1024]{1,0:T(8,128)(2,1)}, u32[]{:S(2)}, u32[]{:S(2)}) collective-permute-start(bf16[2048,1024]{1,0:T(8,128)(2,1)} %bitcast.15.refs_0_), channel_id=1, source_target_pairs={{0,2},{1,3},{2,0},{3,1},{4,6},{5,7},{6,4},{7,5},{8,10},{9,11},{10,... | collective-permute-start | bytes 12582920 | tf_op jit(solution)/shard_map/ppermute | solution.py:23
  233.7 36.3 %collective-permute-start.8 = (bf16[2,256,1024]{2,1,0:T(8,128)(2,1)}, bf16[2,256,1024]{2,1,0:T(8,128)(2,1)}, u32[]{:S(2)}, u32[]{:S(2)}) collective-permute-start(bf16[2,256,1024]{2,1,0:T(8,128)(2,1)} %collective-permute-done.7.refs_4_), channel_id=1, source_target_pairs={{8,0},{12,4},{16,8},{20,12},{9,1},{13,5},{17,9},{21,13},{10,2},{14... | collective-permute-start | bytes 3145736 | tf_op jit(solution)/shard_map/ppermute | solution.py:133
  235.6 55.7 %collective-permute-start.11 = (bf16[2,256,1024]{2,1,0:T(8,128)(2,1)}, bf16[2,256,1024]{2,1,0:T(8,128)(2,1)}, u32[]{:S(2)}, u32[]{:S(2)}) collective-permute-start(bf16[2,256,1024]{2,1,0:T(8,128)(2,1)} %collective-permute-done.4.refs_1_), channel_id=1, source_target_pairs={{8,12},{12,8},{16,20},{20,16},{24,28},{28,24},{9,13},{13,9},{17,21... | collective-permute-start | bytes 3145736 | tf_op jit(solution)/shard_map/ppermute | solution.py:133
  237.6 180.7 %all-to-all-start.1 = ((bf16[8,256,768]{2,1,0:T(8,128)(2,1)}), bf16[8,256,768]{2,1,0:T(8,128)(2,1)S(1)}, u32[]{:S(2)}, u32[]{:S(2)}) async-start(bf16[8,256,768]{2,1,0:T(8,128)(2,1)} %bitcast.52), calls=%async_computation.1 | async-start | bytes 6291456 | tf_op jit(solution)/shard_map/all_to_all | solution.py:282
  257.0 77.3 %collective-permute-start.5 = (bf16[2,256,1024]{2,1,0:T(8,128)(2,1)}, bf16[2,256,1024]{2,1,0:T(8,128)(2,1)}, u32[]{:S(2)}, u32[]{:S(2)}) collective-permute-start(bf16[2,256,1024]{2,1,0:T(8,128)(2,1)} %collective-permute-done.4.refs_1_), channel_id=1, source_target_pairs={{8,16},{12,20},{16,24},{20,28},{9,17},{13,21},{17,25},{21,29},{10,... | collective-permute-start | bytes 3145736 | tf_op jit(solution)/shard_map/ppermute | solution.py:133
  270.0 67.5 %collective-permute-start.35 = (bf16[2,256,1024]{2,1,0:T(8,128)(2,1)}, bf16[2,256,1024]{2,1,0:T(8,128)(2,1)}, u32[]{:S(2)}, u32[]{:S(2)}) collective-permute-start(bf16[2,256,1024]{2,1,0:T(8,128)(2,1)} %collective-permute-done.28.refs_6_), channel_id=1, source_target_pairs={{0,4},{4,0},{1,5},{5,1},{2,6},{6,2},{3,7},{7,3}} | collective-permute-start | bytes 3145736 | tf_op jit(solution)/shard_map/ppermute | solution.py:133
  291.3 48.5 %collective-permute-start.32 = (bf16[2,256,1024]{2,1,0:T(8,128)(2,1)}, bf16[2,256,1024]{2,1,0:T(8,128)(2,1)}, u32[]{:S(2)}, u32[]{:S(2)}) collective-permute-start(bf16[2,256,1024]{2,1,0:T(8,128)(2,1)} %collective-permute-done.25.refs_3_), channel_id=1, source_target_pairs={{24,28},{28,24},{25,29},{29,25},{26,30},{30,26},{27,31},{31,27}} | collective-permute-start | bytes 3145736 | tf_op jit(solution)/shard_map/ppermute | solution.py:133
  334.3 26.4 %collective-permute-start.15 = (bf16[2,256,1024]{2,1,0:T(8,128)(2,1)}, bf16[2,256,1024]{2,1,0:T(8,128)(2,1)}, u32[]{:S(2)}, u32[]{:S(2)}) collective-permute-start(bf16[2,256,1024]{2,1,0:T(8,128)(2,1)} %collective-permute-done.8.refs_5_), channel_id=1, source_target_pairs={{0,4},{4,0},{8,12},{12,8},{1,5},{5,1},{9,13},{13,9},{2,6},{6,2},{1... | collective-permute-start | bytes 3145736 | tf_op jit(solution)/shard_map/ppermute | solution.py:133
  337.5 26.5 %collective-permute-start.9 = (bf16[2,256,1024]{2,1,0:T(8,128)(2,1)}, bf16[2,256,1024]{2,1,0:T(8,128)(2,1)}, u32[]{:S(2)}, u32[]{:S(2)}) collective-permute-start(bf16[2,256,1024]{2,1,0:T(8,128)(2,1)} %collective-permute-done.8.refs_5_), channel_id=1, source_target_pairs={{8,0},{12,4},{9,1},{13,5},{10,2},{14,6},{11,3},{15,7}} | collective-permute-start | bytes 3145736 | tf_op jit(solution)/shard_map/ppermute | solution.py:133
  339.8 25.6 %collective-permute-start.12 = (bf16[2,256,1024]{2,1,0:T(8,128)(2,1)}, bf16[2,256,1024]{2,1,0:T(8,128)(2,1)}, u32[]{:S(2)}, u32[]{:S(2)}) collective-permute-start(bf16[2,256,1024]{2,1,0:T(8,128)(2,1)} %collective-permute-done.5.refs_2_), channel_id=1, source_target_pairs={{16,20},{20,16},{24,28},{28,24},{17,21},{21,17},{25,29},{29,25},{1... | collective-permute-start | bytes 3145736 | tf_op jit(solution)/shard_map/ppermute | solution.py:133
  345.6 68.4 %copy-start.5 = (s32[1,17]{1,0:T(1,128)}, s32[1,17]{1,0:T(1,128)S(1)}, u32[]{:S(2)}) copy-start(s32[1,17]{1,0:T(1,128)S(1)} %add_bitcast_fusion.3.bounds) | copy-start | bytes 208
  360.7 9.4 %collective-permute-start.6 = (bf16[2,256,1024]{2,1,0:T(8,128)(2,1)}, bf16[2,256,1024]{2,1,0:T(8,128)(2,1)}, u32[]{:S(2)}, u32[]{:S(2)}) collective-permute-start(bf16[2,256,1024]{2,1,0:T(8,128)(2,1)} %collective-permute-done.5.refs_2_), channel_id=1, source_target_pairs={{16,24},{20,28},{17,25},{21,29},{18,26},{22,30},{19,27},{23,31}} | collective-permute-start | bytes 3145736 | tf_op jit(solution)/shard_map/ppermute | solution.py:133
  363.3 50.8 %copy-start.9 = (s32[1,17]{1,0:T(1,128)}, s32[1,17]{1,0:T(1,128)S(1)}, u32[]{:S(2)}) copy-start(s32[1,17]{1,0:T(1,128)S(1)} %fusion.1.bounds) | copy-start | bytes 208
  363.4 50.7 %copy-start.6 = (s32[1,17]{1,0:T(1,128)}, s32[1,17]{1,0:T(1,128)S(1)}, u32[]{:S(2)}) copy-start(s32[1,17]{1,0:T(1,128)S(1)} %fusion.bounds) | copy-start | bytes 208
  364.0 82.7 %collective-permute-start.40 = (bf16[2048,1024]{1,0:T(8,128)(2,1)}, bf16[2048,1024]{1,0:T(8,128)(2,1)}, u32[]{:S(2)}, u32[]{:S(2)}) collective-permute-start(bf16[2048,1024]{1,0:T(8,128)(2,1)} %bitcast.15.refs_0_), channel_id=1, source_target_pairs={{0,1},{1,0},{2,3},{3,2},{4,5},{5,4},{6,7},{7,6},{8,9},{9,8},{10,11... | collective-permute-start | bytes 12582920 | tf_op jit(solution)/shard_map/ppermute | solution.py:23
  365.4 80.5 %collective-permute-start.37 = (bf16[1024,1792]{1,0:T(8,128)(2,1)}, bf16[1024,1792]{1,0:T(8,128)(2,1)}, u32[]{:S(2)}, u32[]{:S(2)}) collective-permute-start(bf16[1024,1792]{1,0:T(8,128)(2,1)} %dynamic-slice_bitcast_fusion.1), channel_id=1, source_target_pairs={{0,1},{1,0},{2,3},{3,2},{4,5},{5,4},{6,7},{7,6},{8,9},{9,8},{10,11... | collective-permute-start | bytes 11010056 | tf_op jit(solution)/shard_map/ppermute | solution.py:23
  365.6 48.5 %copy-start.7 = (s32[1,17]{1,0:T(1,128)}, s32[1,17]{1,0:T(1,128)S(1)}, u32[]{:S(2)}) copy-start(s32[1,17]{1,0:T(1,128)S(1)} %add_bitcast_fusion.2.bounds) | copy-start | bytes 208
  370.1 48.1 %collective-permute-start.16 = (bf16[2,256,1024]{2,1,0:T(8,128)(2,1)}, bf16[2,256,1024]{2,1,0:T(8,128)(2,1)}, u32[]{:S(2)}, u32[]{:S(2)}) collective-permute-start(bf16[2,256,1024]{2,1,0:T(8,128)(2,1)} %collective-permute-done.9.refs_6_), channel_id=1, source_target_pairs={{0,4},{4,0},{1,5},{5,1},{2,6},{6,2},{3,7},{7,3}} | collective-permute-start | bytes 3145736 | tf_op jit(solution)/shard_map/ppermute | solution.py:133
  371.7 46.5 %collective-permute-start.13 = (bf16[2,256,1024]{2,1,0:T(8,128)(2,1)}, bf16[2,256,1024]{2,1,0:T(8,128)(2,1)}, u32[]{:S(2)}, u32[]{:S(2)}) collective-permute-start(bf16[2,256,1024]{2,1,0:T(8,128)(2,1)} %collective-permute-done.6.refs_3_), channel_id=1, source_target_pairs={{24,28},{28,24},{25,29},{29,25},{26,30},{30,26},{27,31},{31,27}} | collective-permute-start | bytes 3145736 | tf_op jit(solution)/shard_map/ppermute | solution.py:133
  384.2 117.6 %collective-permute-start.39 = (bf16[2048,1024]{1,0:T(8,128)(2,1)}, bf16[2048,1024]{1,0:T(8,128)(2,1)}, u32[]{:S(2)}, u32[]{:S(2)}) collective-permute-start(bf16[2048,1024]{1,0:T(8,128)(2,1)} %collective-permute-done.38.refs_0_), channel_id=1, source_target_pairs={{0,1},{1,0},{2,3},{3,2},{4,5},{5,4},{6,7},{7,6},{8,9},{9,8},{10,11... | collective-permute-start | bytes 12582920 | tf_op jit(solution)/shard_map/ppermute | solution.py:23
  418.2 83.5 %collective-permute-start.20 = (bf16[1024,1792]{1,0:T(8,128)(2,1)}, bf16[1024,1792]{1,0:T(8,128)(2,1)}, u32[]{:S(2)}, u32[]{:S(2)}) collective-permute-start(bf16[1024,1792]{1,0:T(8,128)(2,1)} %constant_dynamic-slice_fusion.2), channel_id=1, source_target_pairs={{0,1},{1,0},{2,3},{3,2},{4,5},{5,4},{6,7},{7,6},{8,9},{9,8},{10,11... | collective-permute-start | bytes 11010056 | tf_op jit(solution)/shard_map/ppermute | solution.py:23
  418.2 27.7 %copy-start.1 = (bf16[8,256,768]{2,1,0:T(8,128)(2,1)}, bf16[8,256,768]{2,1,0:T(8,128)(2,1)S(1)}, u32[]{:S(2)}) copy-start(bf16[8,256,768]{2,1,0:T(8,128)(2,1)S(1)} %all-to-all-done.1) | copy-start | bytes 9437188
  418.2 69.3 %collective-permute-start.17 = (bf16[2048,768]{1,0:T(8,128)(2,1)S(1)}, bf16[2048,768]{1,0:T(8,128)(2,1)}, u32[]{:S(2)}, u32[]{:S(2)}) collective-permute-start(bf16[2048,768]{1,0:T(8,128)(2,1)S(1)} %bitcast.60), channel_id=1, source_target_pairs={{0,2},{1,3},{2,0},{3,1},{4,6},{5,7},{6,4},{7,5},{8,10},{9,11},{10,... | collective-permute-start | bytes 9437192 | tf_op jit(solution)/shard_map/ppermute | solution.py:23
  445.9 85.9 %collective-permute-start.36 = (bf16[2048,768]{1,0:T(8,128)(2,1)S(1)}, bf16[2048,768]{1,0:T(8,128)(2,1)}, u32[]{:S(2)}, u32[]{:S(2)}) collective-permute-start(bf16[2048,768]{1,0:T(8,128)(2,1)S(1)} %bitcast.61), channel_id=1, source_target_pairs={{0,1},{1,0},{2,3},{3,2},{4,5},{5,4},{6,7},{7,6},{8,9},{9,8},{10,11... | collective-permute-start | bytes 9437192 | tf_op jit(solution)/shard_map/ppermute | solution.py:23
  487.6 72.3 %collective-permute-start.18 = (bf16[2048,768]{1,0:T(8,128)(2,1)}, bf16[2048,768]{1,0:T(8,128)(2,1)}, u32[]{:S(2)}, u32[]{:S(2)}) collective-permute-start(bf16[2048,768]{1,0:T(8,128)(2,1)} %collective-permute-done.17.refs_0_), channel_id=1, source_target_pairs={{0,1},{1,0},{2,3},{3,2},{4,5},{5,4},{6,7},{7,6},{8,9},{9,8},{10,11... | collective-permute-start | bytes 9437192 | tf_op jit(solution)/shard_map/ppermute | solution.py:23
